TPU v7x, 32 devices: a whole 2x2x4 slice. The times are simulated.
32 devices in a mesh: design: 2 (over x), gx: 4 (over y, core), gy: 4 (over z).
Axes of the slice: x: 2, y: 2, z: 4, core: 2. Of those that a mesh axis runs over, the one named last changes fastest.
Arguments:
- e_field: float32 [6, 16, 64, 512], P('design', None, 'gx', 'gy'), parts along dimension 0, may hold values from -6 to 6
- h_field: float32 [6, 16, 64, 512], P('design', None, 'gx', 'gy'), parts along dimension 0, may hold values from -6 to 6
- inverse_permittivity: float32 [32, 64, 512], P('design', 'gx', 'gy'), parts along dimension 0, may hold values from 0.0833 to 1
- monitor_layer: int32 [128, 512], P(('design', 'gx'), 'gy'), parts along dimension 0, may hold values from 0 to 15
- source_layer: int32 [128, 512], P(('design', 'gx'), 'gy'), parts along dimension 0, may hold values from 0 to 15
- residual_far: float32 [4, 2, 2, 256, 256], P('design', None, None, 'gx', 'gy'), parts along dimension 0, may hold values from -6 to 6
Outputs:
- e_forward: float32 [6, 16, 64, 512], P('design', None, 'gx', 'gy'), parts along dimension 0
- far_field: float32 [4, 2, 2, 256, 256], P('design', None, None, 'gx', 'gy'), parts along dimension 0
- e_adjoint: float32 [6, 16, 64, 512], P('design', None, 'gx', 'gy'), parts along dimension 0
There are 2 independent parts, one for each index of `design`. A program takes and returns all parts, laid end to end along the dimension named above; each array names one. Nothing has to cross between parts.
All inputs are finite; a program needn't handle non-finite values.
Results may differ from a plain program's by a relative error of at most 0.0001.
Values sent between devices are 32-bit elements; how exact they have to be, the bound alone decides.
No kernel may reach another device: no remote copies, remote signals or barrier semaphores. Data moves between devices by JAX's collectives and lax.ppermute only.
A program may use at most 64 MiB of HBM per device.

v0:
```python
import math

import jax
import jax.numpy as jnp
from jax import lax
from jax.sharding import PartitionSpec as P

NZ = 16
DIRS = 256


courant = 0.5
omegas = (0.7, 1.3)
factors = (3, 5)
highest = lax.Precision.HIGHEST


def from_behind(value, axis, steps):
    count = lax.axis_size(axis)
    leading, last = (max(0, -steps), min(count, count - steps))
    return lax.ppermute(value, axis, [(source, source + steps) for source in range(leading, last)])


def contract(form, left, right):
    return jnp.einsum(form, left, right, precision=highest)


def ahead(field, along):
    count = field.shape[along]
    widths = [(0, 0)] * field.ndim
    widths[along] = (0, 1)
    return jnp.pad(lax.slice_in_dim(field, 1, count, axis=along), widths)


def behind(field, along):
    count = field.shape[along]
    widths = [(0, 0)] * field.ndim
    widths[along] = (1, 0)
    return jnp.pad(lax.slice_in_dim(field, 0, count - 1, axis=along), widths)


def phase_pair(rows, cols, length):
    cosines = []
    sines = []
    for factor in factors:
        index = jnp.mod((rows[:, None] - DIRS // 2) * cols[None, :] * factor, 4 * length)
        angle = index.astype(jnp.float32) * (2.0 * math.pi / (4 * length))
        cosines.append(jnp.cos(angle))
        sines.append(jnp.sin(angle))
    return (jnp.stack(cosines), jnp.stack(sines))


def step_magnetic(elec, magn):
    face_x = from_behind(jnp.stack([elec[1][:, :1, :], elec[2][:, :1, :]]), "gx", -1)
    face_y = from_behind(jnp.stack([elec[0][:, :, :1], elec[2][:, :, :1]]), "gy", -1)
    next_x1 = jnp.concatenate([elec[1][:, 1:, :], face_x[0]], axis=1)
    next_x2 = jnp.concatenate([elec[2][:, 1:, :], face_x[1]], axis=1)
    next_y0 = jnp.concatenate([elec[0][:, :, 1:], face_y[0]], axis=2)
    next_y2 = jnp.concatenate([elec[2][:, :, 1:], face_y[1]], axis=2)
    curl_x = next_y2 - elec[2] - (ahead(elec[1], 0) - elec[1])
    curl_y = ahead(elec[0], 0) - elec[0] - (next_x2 - elec[2])
    curl_z = next_x1 - elec[1] - (next_y0 - elec[0])
    return magn - courant * jnp.stack([curl_x, curl_y, curl_z])


def step_electric(elec, magn, inverse, current):
    face_x = from_behind(jnp.stack([magn[1][:, -1:, :], magn[2][:, -1:, :]]), "gx", 1)
    face_y = from_behind(jnp.stack([magn[0][:, :, -1:], magn[2][:, :, -1:]]), "gy", 1)
    prev_x1 = jnp.concatenate([face_x[0], magn[1][:, :-1, :]], axis=1)
    prev_x2 = jnp.concatenate([face_x[1], magn[2][:, :-1, :]], axis=1)
    prev_y0 = jnp.concatenate([face_y[0], magn[0][:, :, :-1]], axis=2)
    prev_y2 = jnp.concatenate([face_y[1], magn[2][:, :, :-1]], axis=2)
    curl_x = magn[2] - prev_y2 - (magn[1] - behind(magn[1], 0))
    curl_y = magn[0] - behind(magn[0], 0) - (magn[2] - prev_x2)
    curl_z = magn[1] - prev_x1 - (magn[0] - prev_y0)
    if current is not None:
        curl_x = curl_x - current[0]
        curl_y = curl_y - current[1]
    return elec + courant * inverse[None] * jnp.stack([curl_x, curl_y, curl_z])


def per_device(e_field, h_field, inverse_permittivity, monitor_layer, source_layer, residual_far):
    cells_x = e_field.shape[2]
    cells_y = e_field.shape[3]
    total_x = cells_x * lax.axis_size("gx")
    total_y = cells_y * lax.axis_size("gy")
    global_x = lax.axis_index("gx") * cells_x + jnp.arange(cells_x, dtype=jnp.int32)
    global_y = lax.axis_index("gy") * cells_y + jnp.arange(cells_y, dtype=jnp.int32)
    directions = jnp.arange(DIRS, dtype=jnp.int32)
    elec = e_field
    magn = h_field
    watch = (jnp.arange(NZ, dtype=jnp.int32)[:, None, None] == monitor_layer[None]).astype(
        jnp.float32
    )
    planes = []
    for moment in range(2):
        magn = step_magnetic(elec, magn)
        elec = step_electric(elec, magn, inverse_permittivity, None)
        planes.append(jnp.sum(elec[:2] * watch[None], axis=1))
    e_forward = elec
    spec_real = jnp.stack(
        [math.cos(omega) * planes[0] + math.cos(2 * omega) * planes[1] for omega in omegas]
    )
    spec_imag = jnp.stack(
        [-(math.sin(omega) * planes[0] + math.sin(2 * omega) * planes[1]) for omega in omegas]
    )
    cos_x, sin_x = phase_pair(directions, global_x, total_x)
    cos_y, sin_y = phase_pair(directions, global_y, total_y)
    q_real = contract("fcxy,fby->fcxb", spec_real, cos_y) + contract(
        "fcxy,fby->fcxb", spec_imag, sin_y
    )
    q_imag = contract("fcxy,fby->fcxb", spec_imag, cos_y) - contract(
        "fcxy,fby->fcxb", spec_real, sin_y
    )
    owned = lax.psum_scatter(
        jnp.stack([q_real, q_imag], axis=2), "gy", scatter_dimension=4, tiled=True
    )
    a_real = contract("fax,fcxb->fcab", cos_x, owned[:, :, 0]) + contract(
        "fax,fcxb->fcab", sin_x, owned[:, :, 1]
    )
    a_imag = contract("fax,fcxb->fcab", cos_x, owned[:, :, 1]) - contract(
        "fax,fcxb->fcab", sin_x, owned[:, :, 0]
    )
    summed = lax.psum_scatter(
        jnp.stack([a_real, a_imag], axis=2), "gx", scatter_dimension=3, tiled=True
    )
    far_field = summed * (1.0 / math.sqrt(total_x * total_y))
    piece = lax.all_gather(residual_far, "gy", axis=4, tiled=True)
    rows = jnp.arange(piece.shape[4], dtype=jnp.int32)
    part_cos, part_sin = phase_pair(rows, global_y, total_y)
    u_real = contract("fcab,fby->fcay", piece[:, :, 0], part_cos) - contract(
        "fcab,fby->fcay", piece[:, :, 1], part_sin
    )
    u_imag = contract("fcab,fby->fcay", piece[:, :, 0], part_sin) + contract(
        "fcab,fby->fcay", piece[:, :, 1], part_cos
    )
    mixed = jnp.stack([u_real, u_imag], axis=2)
    piece = lax.all_gather(mixed, "gx", axis=3, tiled=True)
    rows = jnp.arange(piece.shape[3], dtype=jnp.int32)
    part_cos, part_sin = phase_pair(rows, global_x, total_x)
    s_real = contract("fax,fcay->fcxy", part_cos, piece[:, :, 0]) - contract(
        "fax,fcay->fcxy", part_sin, piece[:, :, 1]
    )
    s_imag = contract("fax,fcay->fcxy", part_cos, piece[:, :, 1]) + contract(
        "fax,fcay->fcxy", part_sin, piece[:, :, 0]
    )
    source = jnp.stack([s_real, s_imag], axis=2) / DIRS
    s_real = source[:, :, 0]
    s_imag = source[:, :, 1]
    layers = (jnp.arange(NZ, dtype=jnp.int32)[:, None, None] == source_layer[None]).astype(
        jnp.float32
    )
    elec = jnp.zeros_like(e_field)
    magn = jnp.zeros_like(h_field)
    for moment in range(2):
        tick = moment + 1
        drive = s_real[0] * math.cos(omegas[0] * tick) - s_imag[0] * math.sin(omegas[0] * tick)
        drive = (
            drive + s_real[1] * math.cos(omegas[1] * tick) - s_imag[1] * math.sin(omegas[1] * tick)
        )
        current = layers[None] * drive[:, None]
        magn = step_magnetic(elec, magn)
        elec = step_electric(elec, magn, inverse_permittivity, current)
    return (e_forward, far_field, elec)


def solution(mesh):
    in_specs = (
        P("design", None, "gx", "gy"),
        P("design", None, "gx", "gy"),
        P("design", "gx", "gy"),
        P(("design", "gx"), "gy"),
        P(("design", "gx"), "gy"),
        P("design", None, None, "gx", "gy"),
    )
    out_specs = (
        P("design", None, "gx", "gy"),
        P("design", None, None, "gx", "gy"),
        P("design", None, "gx", "gy"),
    )
    return jax.shard_map(
        per_device, mesh=mesh, in_specs=in_specs, out_specs=out_specs, check_vma=False
    )
```

profile of v0, /device:TPU:0, one launch (start us, length us, event | category | flops | bytes accessed | tf_op | source)
XLA Modules:
  0.0 229.4 jit_solution(10136198741308827661)
XLA Ops:
  15.6 25.9 %all_gather.6 = f32[2,2,2,64,256]{3,2,1,0,4:T(2,128)S(1)} all-gather(f32[2,2,2,64,64]{3,2,1,0,4:T(2,128)S(1)} %copy.993), channel_id=1, replica_groups=mesh['design'=2,'gx'=4,'gy'=4] {'gy'}, dimensions={4}, use_global_device_ids=true | all-gather | bytes 655360 | tf_op jit(solution)/shard_map/all_gather | solution.py:128
  41.5 1.8 fusion.114
  43.3 1.9 copy.1024
  52.5 1.5 collective-permute-start.8
  69.6 1.5 copy.959
  71.1 4.4 %fusion.9 = (f32[1,16,16,128]{2,1,3,0:T(8,128)}, f32[1,16,16,128]{2,1,3,0:T(8,128)}) fusion(f32[16,16,1]{1,0,2:T(8,128)S(1)} %get-tuple-element.134, f32[16,16,127]{1,0,2:T(8,128)} %slice.737, f32[15,16,128]{1,0,2:T(8,128)} %bitcast.405, f32[1,16,16,128]{2,1,3,0:T(8,128)S(1)} %copy.1020, f32[1,16,16,128]{2,1,3,0:T(8,128)S(1)} %copy.1017, ...), kind=kLoop, calls=%fused_computation.19 | loop fusion | flops 262144 | bytes 1163264 | tf_op jit(solution)/shard_map/stack | solution.py:63
  75.5 1.7 copy.961
  79.1 2.9 %fusion.12 = f32[1,16,16,128]{2,1,3,0:T(8,128)} fusion(f32[1,16,16,128]{2,1,3,0:T(8,128)S(1)} %copy.1020, f32[1,16,1,128]{2,1,3,0:T(8,128)} %copy.960, f32[1,16,15,128]{2,1,3,0:T(8,128)S(1)} %copy-done.2, f32[1,16,16,128]{2,1,3,0:T(8,128)S(1)} %copy.1018, f32[1,16,16,1]{2,1,3,0:T(8,128)S(1)} %get-tuple-element.135, f32[1,16,16,127]{2,1,3,0:T(8,128)} %slice_bitcast_fusion.1), kind=kLoop, calls=%fused_computation.24 | loop fusion | flops 163840 | bytes 655360 | tf_op jit(solution)/shard_map/sub | solution.py:62
  82.0 1.7 copy.963
  95.7 4.6 %collective-permute-start.2 = (f32[2,16,16,1]{3,2,1,0:T(8,128)S(1)}, f32[2,16,16,1]{3,2,1,0:T(8,128)S(1)}, u32[]{:S(2)}, u32[]{:S(2)}) collective-permute-start(f32[2,16,16,1]{3,2,1,0:T(8,128)S(1)} %copy.964), channel_id=1, source_target_pairs={{0,1},{1,2},{2,3},{4,5},{5,6},{6,7},{8,9},{9,10},{10,11},{12,13},{... | collective-permute-start | bytes 6152 | tf_op jit(solution)/shard_map/ppermute | solution.py:21
  100.3 2.5 %collective-permute-start.3 = (f32[2,16,1,128]{3,1,2,0:T(8,128)S(1)}, f32[2,16,1,128]{3,1,2,0:T(8,128)S(1)}, u32[]{:S(2)}, u32[]{:S(2)}) collective-permute-start(f32[2,16,1,128]{3,1,2,0:T(8,128)S(1)} %pad_maximum_fusion.12), channel_id=1, source_target_pairs={{0,4},{4,8},{8,12},{1,5},{5,9},{9,13},{2,6},{6,10},{10,14},{3,7},{... | collective-permute-start | bytes 49160 | tf_op jit(solution)/shard_map/ppermute | solution.py:21
  103.1 3.0 %collective-permute-start.10 = (f32[2,16,16,1]{3,2,1,0:T(8,128)S(1)}, f32[2,16,16,1]{3,2,1,0:T(8,128)S(1)}, u32[]{:S(2)}, u32[]{:S(2)}) collective-permute-start(f32[2,16,16,1]{3,2,1,0:T(8,128)S(1)} %copy.991), channel_id=1, source_target_pairs={{0,1},{1,2},{2,3},{4,5},{5,6},{6,7},{8,9},{9,10},{10,11},{12,13},{... | collective-permute-start | bytes 6152 | tf_op jit(solution)/shard_map/ppermute | solution.py:21
  106.1 4.0 %collective-permute-start.11 = (f32[2,16,1,128]{3,1,2,0:T(8,128)S(1)}, f32[2,16,1,128]{3,1,2,0:T(8,128)S(1)}, u32[]{:S(2)}, u32[]{:S(2)}) collective-permute-start(f32[2,16,1,128]{3,1,2,0:T(8,128)S(1)} %pad_maximum_fusion.18), channel_id=1, source_target_pairs={{0,4},{4,8},{8,12},{1,5},{5,9},{9,13},{2,6},{6,10},{10,14},{3,7},{... | collective-permute-start | bytes 49160 | tf_op jit(solution)/shard_map/ppermute | solution.py:21
  115.6 1.4 fusion.14
  128.8 5.1 %collective-permute-done.4 = f32[2,16,16,1]{3,2,1,0:T(8,128)} collective-permute-done((f32[2,16,16,1]{3,2,1,0:T(8,128)}, f32[2,16,16,1]{3,2,1,0:T(8,128)}, u32[]{:S(2)}, u32[]{:S(2)}) %collective-permute-start.4) | collective-permute-done | bytes 2080 | tf_op jit(solution)/shard_map/ppermute | solution.py:21
  134.9 4.5 %collective-permute-done.12 = f32[2,16,16,1]{3,2,1,0:T(8,128)S(1)} collective-permute-done((f32[2,16,16,1]{3,2,1,0:T(8,128)}, f32[2,16,16,1]{3,2,1,0:T(8,128)S(1)}, u32[]{:S(2)}, u32[]{:S(2)}) %collective-permute-start.12) | collective-permute-done | bytes 2080 | tf_op jit(solution)/shard_map/ppermute | solution.py:21
  147.7 4.9 %collective-permute-start.6 = (f32[2,16,16,1]{3,2,1,0:T(8,128)S(1)}, f32[2,16,16,1]{3,2,1,0:T(8,128)}, u32[]{:S(2)}, u32[]{:S(2)}) collective-permute-start(f32[2,16,16,1]{3,2,1,0:T(8,128)S(1)} %copy.972), channel_id=1, source_target_pairs={{0,1},{1,2},{2,3},{4,5},{5,6},{6,7},{8,9},{9,10},{10,11},{12,13},{... | collective-permute-start | bytes 6152 | tf_op jit(solution)/shard_map/ppermute | solution.py:21
  153.2 2.3 %collective-permute-start.7 = (f32[2,16,1,128]{3,1,2,0:T(8,128)}, f32[2,16,1,128]{3,1,2,0:T(8,128)}, u32[]{:S(2)}, u32[]{:S(2)}) collective-permute-start(f32[2,16,1,128]{3,1,2,0:T(8,128)} %pad_maximum_fusion.16), channel_id=1, source_target_pairs={{0,4},{4,8},{8,12},{1,5},{5,9},{9,13},{2,6},{6,10},{10,14},{3,7},{... | collective-permute-start | bytes 49160 | tf_op jit(solution)/shard_map/ppermute | solution.py:21
  156.5 3.4 %collective-permute-start.14 = (f32[2,16,16,1]{3,2,1,0:T(8,128)}, f32[2,16,16,1]{3,2,1,0:T(8,128)S(1)}, u32[]{:S(2)}, u32[]{:S(2)}) collective-permute-start(f32[2,16,16,1]{3,2,1,0:T(8,128)} %copy.1002), channel_id=1, source_target_pairs={{0,1},{1,2},{2,3},{4,5},{5,6},{6,7},{8,9},{9,10},{10,11},{12,13},{... | collective-permute-start | bytes 6152 | tf_op jit(solution)/shard_map/ppermute | solution.py:21
  160.0 4.3 %collective-permute-start.15 = (f32[2,16,1,128]{3,1,2,0:T(8,128)S(1)}, f32[2,16,1,128]{3,1,2,0:T(8,128)S(1)}, u32[]{:S(2)}, u32[]{:S(2)}) collective-permute-start(f32[2,16,1,128]{3,1,2,0:T(8,128)S(1)} %pad_maximum_fusion.22), channel_id=1, source_target_pairs={{0,4},{4,8},{8,12},{1,5},{5,9},{9,13},{2,6},{6,10},{10,14},{3,7},{... | collective-permute-start | bytes 49160 | tf_op jit(solution)/shard_map/ppermute | solution.py:21
  172.2 1.9 reshape.781
  174.2 20.1 %reduce-scatter.7.cloned.1.call-done = f32[64,128]{1,0:T(8,128)} async-done(((f32[256,128]{1,0:T(8,128)}), f32[64,128]{1,0:T(8,128)}) %reduce-scatter.7.cloned.1.call-update) | async-done | bytes 32784
  199.1 1.7 reshape.783
  200.8 20.0 %reduce-scatter.9.cloned.1.call-done = f32[64,512]{1,0:T(8,128)} async-done(((f32[256,512]{1,0:T(8,128)}), f32[64,512]{1,0:T(8,128)}) %reduce-scatter.9.cloned.1.call-update) | async-done | bytes 131088
  (327 shorter events, 87.4 us)
Async XLA Ops:
  7.2 106.4 %all-gather.2.cloned.1.call-start = ((), (), s32[]{:S(2)}) async-start(), calls=%async_computation.2 | async-start | bytes 1310720 | tf_op jit(solution)/shard_map/all_gather | solution.py:138
  9.9 57.5 %collective-permute-start = (f32[2,16,16,1]{2,1,3,0:T(8,128)}, f32[2,16,16,1]{2,1,3,0:T(8,128)}, u32[]{:S(2)}, u32[]{:S(2)}) collective-permute-start(f32[2,16,16,1]{2,1,3,0:T(8,128)} %pad_maximum_fusion.9), channel_id=1, source_target_pairs={{1,0},{2,1},{3,2},{5,4},{6,5},{7,6},{9,8},{10,9},{11,10},{13,12},{... | collective-permute-start | bytes 6152 | tf_op jit(solution)/shard_map/ppermute | solution.py:21
  13.1 55.7 %collective-permute-start.1 = (f32[2,16,1,128]{3,1,2,0:T(8,128)}, f32[2,16,1,128]{3,1,2,0:T(8,128)}, u32[]{:S(2)}, u32[]{:S(2)}) collective-permute-start(f32[2,16,1,128]{3,1,2,0:T(8,128)} %pad_maximum_fusion.10), channel_id=1, source_target_pairs={{4,0},{8,4},{12,8},{5,1},{9,5},{13,9},{6,2},{10,6},{14,10},{7,3},{... | collective-permute-start | bytes 49160 | tf_op jit(solution)/shard_map/ppermute | solution.py:21
  14.5 31.9 %copy-start.59 = (s32[256]{0:T(256)}, s32[256]{0:T(256)S(1)}, u32[]{:S(2)}) copy-start(s32[256]{0:T(256)S(1)} %iota_add_fusion) | copy-start | bytes 3076
  50.0 144.2 %reduce-scatter.7.cloned.1.call-start = ((), (), s32[]{:S(2)}) async-start(), calls=%async_computation.3 | async-start | bytes 163840
  50.6 38.5 %collective-permute-start.9 = (f32[2,16,1,128]{3,1,2,0:T(8,128)}, f32[2,16,1,128]{3,1,2,0:T(8,128)}, u32[]{:S(2)}, u32[]{:S(2)}) collective-permute-start(f32[2,16,1,128]{3,1,2,0:T(8,128)} %stack.342), channel_id=1, source_target_pairs={{4,0},{8,4},{12,8},{5,1},{9,5},{13,9},{6,2},{10,6},{14,10},{7,3},{... | collective-permute-start | bytes 49160 | tf_op jit(solution)/shard_map/ppermute | solution.py:21
  52.5 13.5 %collective-permute-start.8 = (f32[2,16,16,1]{2,1,3,0:T(8,128)}, f32[2,16,16,1]{2,1,3,0:T(8,128)}, u32[]{:S(2)}, u32[]{:S(2)}) collective-permute-start(f32[2,16,16,1]{2,1,3,0:T(8,128)} %stack.340), channel_id=1, source_target_pairs={{1,0},{2,1},{3,2},{5,4},{6,5},{7,6},{9,8},{10,9},{11,10},{13,12},{... | collective-permute-start | bytes 6152 | tf_op jit(solution)/shard_map/ppermute | solution.py:21
  77.2 6.4 %copy-start.18 = (f32[1,16,16,128]{3,2,1,0:T(8,128)}, f32[1,16,16,128]{3,2,1,0:T(8,128)S(1)}, u32[]{:S(2)}) copy-start(f32[1,16,16,128]{3,2,1,0:T(8,128)S(1)} %copy.961) | copy-start | bytes 393220
  77.7 6.0 %copy-start.20 = (f32[1,16,16,128]{3,2,1,0:T(8,128)}, f32[1,16,16,128]{3,2,1,0:T(8,128)S(1)}, u32[]{:S(2)}) copy-start(f32[1,16,16,128]{3,2,1,0:T(8,128)S(1)} %copy.962) | copy-start | bytes 393220
  95.7 14.4 %collective-permute-start.2 = (f32[2,16,16,1]{3,2,1,0:T(8,128)S(1)}, f32[2,16,16,1]{3,2,1,0:T(8,128)S(1)}, u32[]{:S(2)}, u32[]{:S(2)}) collective-permute-start(f32[2,16,16,1]{3,2,1,0:T(8,128)S(1)} %copy.964), channel_id=1, source_target_pairs={{0,1},{1,2},{2,3},{4,5},{5,6},{6,7},{8,9},{9,10},{10,11},{12,13},{... | collective-permute-start | bytes 6152 | tf_op jit(solution)/shard_map/ppermute | solution.py:21
  100.3 11.0 %collective-permute-start.3 = (f32[2,16,1,128]{3,1,2,0:T(8,128)S(1)}, f32[2,16,1,128]{3,1,2,0:T(8,128)S(1)}, u32[]{:S(2)}, u32[]{:S(2)}) collective-permute-start(f32[2,16,1,128]{3,1,2,0:T(8,128)S(1)} %pad_maximum_fusion.12), channel_id=1, source_target_pairs={{0,4},{4,8},{8,12},{1,5},{5,9},{9,13},{2,6},{6,10},{10,14},{3,7},{... | collective-permute-start | bytes 49160 | tf_op jit(solution)/shard_map/ppermute | solution.py:21
  103.1 8.2 %collective-permute-start.10 = (f32[2,16,16,1]{3,2,1,0:T(8,128)S(1)}, f32[2,16,16,1]{3,2,1,0:T(8,128)S(1)}, u32[]{:S(2)}, u32[]{:S(2)}) collective-permute-start(f32[2,16,16,1]{3,2,1,0:T(8,128)S(1)} %copy.991), channel_id=1, source_target_pairs={{0,1},{1,2},{2,3},{4,5},{5,6},{6,7},{8,9},{9,10},{10,11},{12,13},{... | collective-permute-start | bytes 6152 | tf_op jit(solution)/shard_map/ppermute | solution.py:21
  106.1 5.3 %collective-permute-start.11 = (f32[2,16,1,128]{3,1,2,0:T(8,128)S(1)}, f32[2,16,1,128]{3,1,2,0:T(8,128)S(1)}, u32[]{:S(2)}, u32[]{:S(2)}) collective-permute-start(f32[2,16,1,128]{3,1,2,0:T(8,128)S(1)} %pad_maximum_fusion.18), channel_id=1, source_target_pairs={{0,4},{4,8},{8,12},{1,5},{5,9},{9,13},{2,6},{6,10},{10,14},{3,7},{... | collective-permute-start | bytes 49160 | tf_op jit(solution)/shard_map/ppermute | solution.py:21
  122.7 11.3 %collective-permute-start.4 = (f32[2,16,16,1]{3,2,1,0:T(8,128)}, f32[2,16,16,1]{3,2,1,0:T(8,128)}, u32[]{:S(2)}, u32[]{:S(2)}) collective-permute-start(f32[2,16,16,1]{3,2,1,0:T(8,128)} %copy.968), channel_id=1, source_target_pairs={{1,0},{2,1},{3,2},{5,4},{6,5},{7,6},{9,8},{10,9},{11,10},{13,12},{... | collective-permute-start | bytes 6152 | tf_op jit(solution)/shard_map/ppermute | solution.py:21
  124.0 15.5 %collective-permute-start.5 = (f32[2,16,1,128]{3,1,2,0:T(8,128)S(1)}, f32[2,16,1,128]{3,1,2,0:T(8,128)S(1)}, u32[]{:S(2)}, u32[]{:S(2)}) collective-permute-start(f32[2,16,1,128]{3,1,2,0:T(8,128)S(1)} %pad_maximum_fusion.14), channel_id=1, source_target_pairs={{4,0},{8,4},{12,8},{5,1},{9,5},{13,9},{6,2},{10,6},{14,10},{7,3},{... | collective-permute-start | bytes 49160 | tf_op jit(solution)/shard_map/ppermute | solution.py:21
  126.2 13.2 %collective-permute-start.12 = (f32[2,16,16,1]{3,2,1,0:T(8,128)}, f32[2,16,16,1]{3,2,1,0:T(8,128)S(1)}, u32[]{:S(2)}, u32[]{:S(2)}) collective-permute-start(f32[2,16,16,1]{3,2,1,0:T(8,128)} %copy.998), channel_id=1, source_target_pairs={{1,0},{2,1},{3,2},{5,4},{6,5},{7,6},{9,8},{10,9},{11,10},{13,12},{... | collective-permute-start | bytes 6152 | tf_op jit(solution)/shard_map/ppermute | solution.py:21
  127.5 15.6 %collective-permute-start.13 = (f32[2,16,1,128]{3,1,2,0:T(8,128)S(1)}, f32[2,16,1,128]{3,1,2,0:T(8,128)S(1)}, u32[]{:S(2)}, u32[]{:S(2)}) collective-permute-start(f32[2,16,1,128]{3,1,2,0:T(8,128)S(1)} %pad_maximum_fusion.20), channel_id=1, source_target_pairs={{4,0},{8,4},{12,8},{5,1},{9,5},{13,9},{6,2},{10,6},{14,10},{7,3},{... | collective-permute-start | bytes 49160 | tf_op jit(solution)/shard_map/ppermute | solution.py:21
  147.4 5.2 %copy-start.51 = (f32[16,1,128]{2,1,0:T(1,128)S(1)}, f32[16,1,128]{2,1,0:T(1,128)}, u32[]{:S(2)}) copy-start(f32[16,1,128]{2,1,0:T(1,128)} %slice.792) | copy-start | bytes 24580
  147.4 5.2 %copy-start.52 = (f32[16,1,128]{2,1,0:T(1,128)S(1)}, f32[16,1,128]{2,1,0:T(1,128)}, u32[]{:S(2)}) copy-start(f32[16,1,128]{2,1,0:T(1,128)} %slice.793) | copy-start | bytes 24580
  147.7 16.6 %collective-permute-start.6 = (f32[2,16,16,1]{3,2,1,0:T(8,128)S(1)}, f32[2,16,16,1]{3,2,1,0:T(8,128)}, u32[]{:S(2)}, u32[]{:S(2)}) collective-permute-start(f32[2,16,16,1]{3,2,1,0:T(8,128)S(1)} %copy.972), channel_id=1, source_target_pairs={{0,1},{1,2},{2,3},{4,5},{5,6},{6,7},{8,9},{9,10},{10,11},{12,13},{... | collective-permute-start | bytes 6152 | tf_op jit(solution)/shard_map/ppermute | solution.py:21
  153.2 12.2 %collective-permute-start.7 = (f32[2,16,1,128]{3,1,2,0:T(8,128)}, f32[2,16,1,128]{3,1,2,0:T(8,128)}, u32[]{:S(2)}, u32[]{:S(2)}) collective-permute-start(f32[2,16,1,128]{3,1,2,0:T(8,128)} %pad_maximum_fusion.16), channel_id=1, source_target_pairs={{0,4},{4,8},{8,12},{1,5},{5,9},{9,13},{2,6},{6,10},{10,14},{3,7},{... | collective-permute-start | bytes 49160 | tf_op jit(solution)/shard_map/ppermute | solution.py:21
  156.5 8.8 %collective-permute-start.14 = (f32[2,16,16,1]{3,2,1,0:T(8,128)}, f32[2,16,16,1]{3,2,1,0:T(8,128)S(1)}, u32[]{:S(2)}, u32[]{:S(2)}) collective-permute-start(f32[2,16,16,1]{3,2,1,0:T(8,128)} %copy.1002), channel_id=1, source_target_pairs={{0,1},{1,2},{2,3},{4,5},{5,6},{6,7},{8,9},{9,10},{10,11},{12,13},{... | collective-permute-start | bytes 6152 | tf_op jit(solution)/shard_map/ppermute | solution.py:21
  160.0 6.2 %collective-permute-start.15 = (f32[2,16,1,128]{3,1,2,0:T(8,128)S(1)}, f32[2,16,1,128]{3,1,2,0:T(8,128)S(1)}, u32[]{:S(2)}, u32[]{:S(2)}) collective-permute-start(f32[2,16,1,128]{3,1,2,0:T(8,128)S(1)} %pad_maximum_fusion.22), channel_id=1, source_target_pairs={{0,4},{4,8},{8,12},{1,5},{5,9},{9,13},{2,6},{6,10},{10,14},{3,7},{... | collective-permute-start | bytes 49160 | tf_op jit(solution)/shard_map/ppermute | solution.py:21
  174.1 46.7 %reduce-scatter.9.cloned.1.call-start = ((), (), s32[]{:S(2)}) async-start(), calls=%async_computation.4 | async-start | bytes 655360
  (57 other events, 81.5 us)
Sparse Core Ops, SparseCore 0:
  50.1 18.6 all-gather.1
  174.3 19.9 reduce-scatter.6
  201.0 19.7 reduce-scatter.8
where the time goes:
time: 231 us; the launch traced here: 229 us
  local copies, waits for them, and re-layouts  71.8 us (31%)
  waiting for transfers between devices  50.9 us (22%)
  starting transfers between devices  39.6 us (17%)
  blocking collectives  25.9 us (11%)
  other arithmetic  17.8 us (8%)
  between operations  15.1 us (7%)
  matrix products  8.32 us (4%)
    unnamed x5, waiting for transfers between devices  40.1 us
    ppermute x16, starting transfers between devices, from_behind(): lax.ppermute(value, axis, [(source, source + steps) for source in range(l...  39.4 us
    unnamed x142, local copies, waits for them, and re-layouts  30 us
    all_gather x1, blocking collectives, per_device(): piece = lax.all_gather(residual_far, 'gy', axis=4, tiled=True)  25.9 us
    ppermute x16, waiting for transfers between devices, from_behind(): lax.ppermute(value, axis, [(source, source + steps) for source in range(l...  10.8 us
    dot_general x16, matrix products, contract(): return jnp.einsum(form, left, right, precision=highest)  8.32 us
    another operation x5, other arithmetic, step_magnetic(): return magn - courant * jnp.stack([curl_x, curl_y, curl_z])  5.85 us
  transfers between devices with their start and end apart: 19, of which 5 were waited for; matrix products, arithmetic and copies ran while one was open for 26% of the time, Pallas kernels for 0%

commit v1 on v0

v1 whole, which is shorter than its diff:
```python
import functools
import math

import jax
import jax.numpy as jnp
from jax import lax
from jax.experimental import pallas as pl
from jax.experimental.pallas import tpu as pltpu
from jax.sharding import PartitionSpec as P

NZ = 16
DIRS = 256
HALF = 0.5
OMEGAS = (0.7, 1.3)
FACTORS = (3, 5)
HIGHEST = lax.Precision.HIGHEST
F32 = jnp.float32
LANES = 128
GROUP = 8


def iota(shape, dim):
    return lax.broadcasted_iota(jnp.int32, shape, dim)


def cos_turn(index, length):
    bits = length.bit_length() - 1
    quadrant = lax.shift_right_arithmetic(index + length // 2, bits)
    rest = index - lax.shift_left(quadrant, bits)
    angle = rest.astype(F32) * (0.5 * math.pi / length)
    sq = angle * angle
    cosine = 1.0 + sq * (-0.5 + sq * (1 / 24 + sq * (-1 / 720 + sq * (1 / 40320))))
    sine = angle * (1.0 + sq * (-1 / 6 + sq * (1 / 120 + sq * (-1 / 5040 + sq * (1 / 362880)))))
    value = jnp.where((quadrant & 1) == 1, sine, cosine)
    return jnp.where(((quadrant + 1) & 2) == 2, -value, value)


def dot(left, right):
    return jnp.dot(left, right, precision=HIGHEST, preferred_element_type=F32)


def swap(value, half):
    if 2 * half == LANES:
        return pltpu.roll(value, half, 1)
    return jnp.concatenate([value[:, half:], value[:, :half]], axis=1)


def call(kernel, name, out, scratch=()):
    single = isinstance(out[0], int)
    shapes = [jax.ShapeDtypeStruct(s, F32) for s in ([out] if single else out)]
    return pl.pallas_call(
        kernel,
        out_shape=shapes[0] if single else tuple(shapes),
        scratch_shapes=list(scratch),
        name=name,
    )


def pack_edges(e, h, k, layer, up, down, own, *, cx):
    def rows(ref, count, x, first=0):
        return ref[pl.ds(first * NZ * cx + x, count * NZ, stride=cx), :]

    up[0 : 3 * NZ] = rows(e, 3, cx - 1)
    up[3 * NZ : 6 * NZ] = rows(h, 3, cx - 1)
    up[6 * NZ : 7 * NZ] = rows(k, 1, cx - 1)
    up[7 * NZ : 10 * NZ] = rows(e, 3, cx - 2)
    up[10 * NZ : 12 * NZ] = rows(h, 2, cx - 2, 1)
    down[0 : 3 * NZ] = rows(e, 3, 0)
    down[3 * NZ : 6 * NZ] = rows(h, 3, 0)
    down[6 * NZ : 7 * NZ] = rows(k, 1, 0)
    down[7 * NZ : 9 * NZ] = rows(e, 2, 1, 1)
    lane = iota((cx, LANES), 1)
    width = e.shape[1]

    def shifted(plane, amount):
        return pltpu.roll(plane, amount % width, 1)[:, :LANES]

    for field in range(7):
        ref = (e, h, k)[field // 3]
        base = (field % 3) * NZ
        packed = jnp.zeros((cx, LANES), F32)
        for z in range(NZ):
            plane = ref[(base + z) * cx : (base + z + 1) * cx, :]
            hit = (lane >= GROUP * z) & (lane < GROUP * z + 4)
            packed = jnp.where(hit, shifted(plane, GROUP * z + 2), packed)
        own[field * cx : (field + 1) * cx] = packed
    layers = layer[...].astype(F32)
    packed = jnp.where(lane < 4, shifted(layers, 2), 0.0)
    for amount in (8, 16, 32, 64):
        packed = packed + pltpu.roll(packed, amount, 1)
    own[7 * cx : 8 * cx] = packed
    for field in range(8):
        up[12 * NZ + 2 * field : 12 * NZ + 2 * field + 2] = own[field * cx + cx - 2 : field * cx + cx]
        down[9 * NZ + 2 * field : 9 * NZ + 2 * field + 2] = own[field * cx : field * cx + 2]
    up[12 * NZ + 16 : 12 * NZ + 24] = jnp.broadcast_to(layers[cx - 1 : cx, :], (8, width))
    down[9 * NZ + 16 : 9 * NZ + 24] = jnp.broadcast_to(layers[0:1, :], (8, width))


def pack_strips(own, before, after, up, down, ext, *, cx):
    rows = cx + 8
    first = lax.axis_index("gx") == 0
    last = lax.axis_index("gx") == lax.axis_size("gx") - 1
    lane = iota((rows, LANES), 1) % GROUP
    packed = [[None, None], [None, None]]
    for field in range(8):
        base = field * rows
        ext[base : base + cx] = own[field * cx : (field + 1) * cx]
        ext[base + cx : base + rows] = jnp.zeros((8, LANES), F32)
        late = after[9 * NZ + 2 * field : 9 * NZ + 2 * field + 2]
        ext[base + cx : base + cx + 2] = jnp.where(last, 0.0, late)
        early = before[12 * NZ + 2 * field : 12 * NZ + 2 * field + 2]
        ext[base + rows - 2 : base + rows] = jnp.where(first, 0.0, early)
        strip = ext[base : base + rows]
        group, slot = divmod(field, 4)
        hit = lane // 2 == slot
        for side, amount in ((0, 2 * slot), (1, 2 * slot - 2)):
            moved = pltpu.roll(strip, amount % LANES, 1) if amount else strip
            old = packed[side][group]
            packed[side][group] = moved if old is None else jnp.where(hit, moved, old)
    for group in range(2):
        up[group * rows : (group + 1) * rows] = packed[0][group]
        down[group * rows : (group + 1) * rows] = packed[1][group]


def forward(
    e, h, k, layer, monitor, before, after, own, left, right,
    out, planes, kext, kstrip, lext, lstrip, fe, fh, *, cx
):
    rows = cx + 8
    gx, gy = lax.axis_index("gx"), lax.axis_index("gy")
    first_x, last_x = gx == 0, gx == lax.axis_size("gx") - 1
    first_y, last_y = gy == 0, gy == lax.axis_size("gy") - 1
    width = e.shape[1]
    for dst, src, count in ((fe, e, 3 * NZ), (fh, h, 3 * NZ), (kext, k, NZ)):
        for p in range(count):
            dst[p * rows : p * rows + cx] = src[p * cx : (p + 1) * cx]

    def put(dst, plane, count, row, value, outside):
        dst[pl.ds(plane * rows + row, count, stride=rows), :] = jnp.where(outside, 0.0, value)

    put(fe, 0, 3 * NZ, cx, after[0 : 3 * NZ], last_x)
    put(fh, 0, 3 * NZ, cx, after[3 * NZ : 6 * NZ], last_x)
    put(kext, 0, NZ, cx, after[6 * NZ : 7 * NZ], last_x)
    put(fe, NZ, 2 * NZ, cx + 1, after[7 * NZ : 9 * NZ], last_x)
    put(fe, 0, 3 * NZ, rows - 1, before[0 : 3 * NZ], first_x)
    put(fh, 0, 3 * NZ, rows - 1, before[3 * NZ : 6 * NZ], first_x)
    put(kext, 0, NZ, rows - 1, before[6 * NZ : 7 * NZ], first_x)
    put(fe, 0, 3 * NZ, rows - 2, before[7 * NZ : 10 * NZ], first_x)
    put(fh, NZ, 2 * NZ, rows - 2, before[10 * NZ : 12 * NZ], first_x)
    lext[0:cx] = layer[...].astype(F32)
    lext[cx:rows] = after[9 * NZ + 16 : 9 * NZ + 24]
    lext[rows - 1 : rows] = before[12 * NZ + 16 : 12 * NZ + 17]

    lane = iota((rows, LANES), 1)
    column = lane % GROUP
    strips = []
    for field in range(8):
        group, slot = divmod(field, 4)
        mine = own[field * rows : (field + 1) * rows]
        low = jnp.where(first_y, 0.0, left[group * rows : (group + 1) * rows])
        high = jnp.where(last_y, 0.0, right[group * rows : (group + 1) * rows])
        low = pltpu.roll(low, (-2 * slot) % LANES, 1) if slot else low
        high = pltpu.roll(high, (6 - 2 * slot) % LANES, 1) if slot != 3 else high
        value = jnp.where(column < 4, mine, pltpu.roll(mine, 4, 1))
        value = jnp.where(column < 2, low, jnp.where(column >= 6, high, value))
        strips.append(value)
    kstrip[...] = strips[6]
    lstrip[...] = strips[7]
    es, hs, ks = strips[0:3], strips[3:6], HALF * strips[6]

    row = iota((rows, width), 0)
    inside = jnp.logical_not(first_x & (row >= rows - 2))
    row = iota((rows, LANES), 0)
    inside_strip = jnp.logical_not((first_x & (row >= rows - 2)) | (first_y & (column < 2)))
    wide_lane = iota((rows, width), 1)
    shown = monitor[...]

    def next_x(v):
        return pltpu.roll(v, rows - 1, 0)

    def prev_x(v):
        return pltpu.roll(v, 1, 0)

    def strip_to(strip, source, target):
        moved = pltpu.roll(strip, (target - source) % LANES, 1)
        if width == LANES:
            return moved
        return jnp.concatenate([moved] * (width // LANES), axis=1)

    def next_y(v, strip, z):
        edge = strip_to(strip, GROUP * z + 6, (width - 1) % LANES)
        return jnp.where(wide_lane == width - 1, edge, pltpu.roll(v, width - 1, 1))

    def prev_y(v, strip, z):
        edge = strip_to(strip, GROUP * z + 1, 0)
        return jnp.where(wide_lane == 0, edge, pltpu.roll(v, 1, 1))

    def strip_next_y(v):
        return pltpu.roll(v, LANES - 1, 1)

    def strip_prev_y(v):
        return pltpu.roll(v, 1, 1)

    def strip_next_z(v):
        return jnp.where(lane >= LANES - GROUP, 0.0, pltpu.roll(v, LANES - GROUP, 1))

    def strip_prev_z(v):
        return jnp.where(lane < GROUP, 0.0, pltpu.roll(v, GROUP, 1))

    def load(ref, comp, z):
        p = comp * NZ + z
        return ref[p * rows : (p + 1) * rows]

    for moment in range(2):
        ex, ey, ez = es
        hx, hy, hz = hs
        hx = hx - HALF * ((strip_next_y(ez) - ez) - (strip_next_z(ey) - ey))
        hy = hy - HALF * ((strip_next_z(ex) - ex) - (next_x(ez) - ez))
        hz = hz - HALF * ((next_x(ey) - ey) - (strip_next_y(ex) - ex))
        new_h = [jnp.where(inside_strip, v, 0.0) for v in (hx, hy, hz)]
        hx, hy, hz = new_h
        new_e = [
            ex + ks * ((hz - strip_prev_y(hz)) - (hy - strip_prev_z(hy))),
            ey + ks * ((hx - strip_prev_z(hx)) - (hz - prev_x(hz))),
            ez + ks * ((hy - prev_x(hy)) - (hx - strip_prev_y(hx))),
        ]
        seen_x = jnp.zeros((cx, width), F32)
        seen_y = jnp.zeros((cx, width), F32)
        zero = jnp.zeros((rows, width), F32)
        under_x, under_y = zero, zero
        ex, ey, ez = (load(fe, c, 0) for c in range(3))
        for z in range(NZ):
            above = [load(fe, c, z + 1) for c in range(3)] if z + 1 < NZ else [zero] * 3
            hx, hy, hz = (load(fh, c, z) for c in range(3))
            hx = hx - HALF * ((next_y(ez, es[2], z) - ez) - (above[1] - ey))
            hy = hy - HALF * ((above[0] - ex) - (next_x(ez) - ez))
            hz = hz - HALF * ((next_x(ey) - ey) - (next_y(ex, es[0], z) - ex))
            hx, hy, hz = (jnp.where(inside, v, 0.0) for v in (hx, hy, hz))
            kz = HALF * kext[z * rows : (z + 1) * rows]
            ex = ex + kz * ((hz - prev_y(hz, new_h[2], z)) - (hy - under_y))
            ey = ey + kz * ((hx - under_x) - (hz - prev_x(hz)))
            ez = ez + kz * ((hy - prev_x(hy)) - (hx - prev_y(hx, new_h[0], z)))
            hit = shown == z
            seen_x = jnp.where(hit, ex[:cx], seen_x)
            seen_y = jnp.where(hit, ey[:cx], seen_y)
            for c, (ev, hv) in enumerate(((ex, hx), (ey, hy), (ez, hz))):
                p = c * NZ + z
                if moment == 0:
                    fe[p * rows : (p + 1) * rows] = ev
                    fh[p * rows : (p + 1) * rows] = hv
                else:
                    out[p * cx : (p + 1) * cx] = ev[:cx]
            under_x, under_y = hx, hy
            ex, ey, ez = above
        planes[2 * moment * cx : (2 * moment + 1) * cx] = seen_x
        planes[(2 * moment + 1) * cx : (2 * moment + 2) * cx] = seen_y
        es, hs = new_e, new_h


def tables(far_table, source_table, *, cy, dirs, count):
    gy = lax.axis_index("gy")
    length = cy * count
    wide = 2 * dirs
    for s in range(count):
        sender = (gy - s + count) % count
        for f, factor in enumerate(FACTORS):
            y = sender * cy + iota((cy, wide), 0)
            lane = iota((cy, wide), 1)
            b = gy * dirs + lane % dirs
            turn = (b - DIRS // 2) * factor * y - jnp.where(lane >= dirs, length, 0)
            far_table[s * cy : (s + 1) * cy, f * wide : (f + 1) * wide] = cos_turn(turn, length)
            line = iota((wide, cy + LANES), 0)
            lane = iota((wide, cy + LANES), 1)
            near = lane % GROUP
            near = jnp.where(near < 4, near - 2, near + cy - 6)
            y = gy * cy + jnp.where(lane < cy, lane, near)
            b = sender * dirs + line % dirs
            turn = (b - DIRS // 2) * factor * y + jnp.where(line >= dirs, length, 0)
            base = (s * 2 + f) * wide
            source_table[base : base + wide] = cos_turn(turn, length) * (1.0 / DIRS)


def project_y(*refs, cx, cy, dirs, count):
    blocks, table, out = refs[:count], refs[count], refs[count + 1]
    total = None
    for s in range(count):
        part = dot(blocks[s][...], table[s * cy : (s + 1) * cy])
        total = part if total is None else total + part
    wide = 2 * dirs
    sign = jnp.where(iota((2 * cx, wide), 1) < dirs, 1.0, -1.0)
    for f, omega in enumerate(OMEGAS):
        value = None
        for moment in range(2):
            tick = omega * (moment + 1)
            part = total[2 * cx * moment : 2 * cx * (moment + 1), f * wide : (f + 1) * wide]
            part = math.cos(tick) * (part * sign) - math.sin(tick) * swap(part, dirs)
            value = part if value is None else value + part
        out[f * 2 * cx : (f + 1) * 2 * cx] = value


def project_x(*refs, cx, dirs_x, dirs_y, count, scale):
    blocks, out = refs[:count], refs[count]
    gx = lax.axis_index("gx")
    length = cx * count
    wide = 2 * dirs_y
    lane = iota((dirs_x, 2 * length), 1)
    a = gx * dirs_x + iota((dirs_x, 2 * length), 0)
    slot = lane % length
    x = (gx - slot // cx + count) % count * cx + slot % cx
    sign = jnp.where(iota((length, wide), 1) < dirs_y, 1.0, -1.0)
    for f, factor in enumerate(FACTORS):
        turn = (a - DIRS // 2) * factor * x - jnp.where(lane >= length, length, 0)
        table = cos_turn(turn, length) * scale
        for c in range(2):
            base = (2 * f + c) * cx
            value = jnp.concatenate([ref[base : base + cx] for ref in blocks], axis=0)
            value = jnp.concatenate([value, swap(value, dirs_y) * sign], axis=0)
            field = dot(table, value)
            out[f, c, 0] = field[:, :dirs_y]
            out[f, c, 1] = field[:, dirs_y:]


def spread_x(residual, *outs, cx, dirs_x, dirs_y, count):
    gx = lax.axis_index("gx")
    length = cx * count
    rows = cx + 8
    lane = iota((count * rows, 2 * dirs_x), 1)
    line = iota((count * rows, 2 * dirs_x), 0)
    slot = line % rows
    slot = jnp.where(slot >= cx + 4, slot - rows, slot)
    x = (gx + line // rows) % count * cx + slot
    a = gx * dirs_x + lane % dirs_x
    for f, factor in enumerate(FACTORS):
        turn = (a - DIRS // 2) * factor * x - jnp.where(lane >= dirs_x, length, 0)
        table = cos_turn(turn, length)
        for c in range(2):
            real, imag = residual[f, c, 0], residual[f, c, 1]
            value = jnp.concatenate(
                [jnp.concatenate([real, imag], axis=1), jnp.concatenate([-imag, real], axis=1)], axis=0
            )
            part = dot(table, value)
            pair = 2 * f + c
            for s in range(count):
                base = s * rows
                outs[s][pair * cx : (pair + 1) * cx] = part[base : base + cx]
                edge = 4 * cx + 2 * pair
                outs[s][edge : edge + 1] = part[base + cx : base + cx + 1]
                outs[s][edge + 1 : edge + 2] = part[base + rows - 1 : base + rows]


def adjoint(*refs, cx, cy, dirs, count):
    blocks = refs[:count]
    table, kext, kstrip, lext, lstrip, out = refs[count : count + 6]
    rows = cx + 8
    wide = 2 * dirs
    first_x, first_y = lax.axis_index("gx") == 0, lax.axis_index("gy") == 0
    sign = jnp.where(iota((rows, wide), 1) < dirs, -1.0, 1.0)
    drive = None
    for s in range(count):
        for f, omega in enumerate(OMEGAS):
            parts = [[], []]
            for c in range(2):
                pair = 2 * f + c
                edge = 4 * cx + 2 * pair
                value = jnp.concatenate(
                    [
                        blocks[s][pair * cx : (pair + 1) * cx],
                        blocks[s][edge : edge + 1],
                        jnp.zeros((6, wide), F32),
                        blocks[s][edge + 1 : edge + 2],
                    ],
                    axis=0,
                )
                turned = swap(value, dirs) * sign
                for moment in range(2):
                    tick = omega * (moment + 1)
                    parts[moment].append(math.cos(tick) * value + math.sin(tick) * turned)
            left = jnp.concatenate(parts[0] + parts[1], axis=0)
            base = (s * 2 + f) * wide
            part = dot(left, table[base : base + wide])
            drive = part if drive is None else drive + part
    first = [-HALF * drive[c * rows : (c + 1) * rows] for c in range(2)]
    second = [drive[(2 + c) * rows : (2 + c) * rows + cx, :cy] for c in range(2)]
    ax, ay = (v[:, :cy] for v in first)
    sx, sy = (v[:, cy:] for v in first)
    row = iota((rows, cy), 0)
    inside = jnp.logical_not(first_x & (row >= rows - 2))
    lane = iota((rows, LANES), 1)
    row = iota((rows, LANES), 0)
    inside_strip = jnp.logical_not((first_x & (row >= rows - 2)) | (first_y & (lane % GROUP < 2)))
    wide_lane = iota((rows, cy), 1)
    layer = lext[...]

    hit = lstrip[...] == (lane // GROUP).astype(F32)
    ks = kstrip[...]
    sx = jnp.where(hit, sx * ks, 0.0)
    sy = jnp.where(hit, sy * ks, 0.0)

    def next_z(v):
        return jnp.where(lane >= LANES - GROUP, 0.0, pltpu.roll(v, LANES - GROUP, 1))

    def next_x(v):
        return pltpu.roll(v, rows - 1, 0)

    def prev_x(v):
        return pltpu.roll(v, 1, 0)

    def strip_to(strip, source, target):
        moved = pltpu.roll(strip, (target - source) % LANES, 1)
        if cy == LANES:
            return moved
        return jnp.concatenate([moved] * (cy // LANES), axis=1)

    hsx = jnp.where(inside_strip, HALF * (next_z(sy) - sy), 0.0)
    hsz = -HALF * ((next_x(sy) - sy) - (pltpu.roll(sx, LANES - 1, 1) - sx))
    hsz = jnp.where(inside_strip, hsz, 0.0)
    zero = jnp.zeros((rows, cy), F32)
    under_x, under_y = zero, zero

    def source(z):
        kz = kext[z * rows : (z + 1) * rows]
        hit = layer == float(z)
        return jnp.where(hit, ax * kz, 0.0), jnp.where(hit, ay * kz, 0.0)

    def prev_y(v, strip, z):
        edge = strip_to(strip, GROUP * z + 1, 0)
        return jnp.where(wide_lane == 0, edge, pltpu.roll(v, 1, 1))

    ex, ey = source(0)
    for z in range(NZ):
        above_x, above_y = source(z + 1) if z + 1 < NZ else (zero, zero)
        hx = HALF * (above_y - ey)
        hy = -HALF * (above_x - ex)
        edge = strip_to(sx, GROUP * z + 6, (cy - 1) % LANES)
        right = jnp.where(wide_lane == cy - 1, edge, pltpu.roll(ex, cy - 1, 1))
        hz = -HALF * ((next_x(ey) - ey) - (right - ex))
        hx, hy, hz = (jnp.where(inside, v, 0.0) for v in (hx, hy, hz))
        kz = HALF * kext[z * rows : z * rows + cx]
        hit = layer[:cx] == float(z)
        jx = jnp.where(hit, second[0], 0.0)
        jy = jnp.where(hit, second[1], 0.0)
        curl_x = (hz - prev_y(hz, hsz, z)) - (hy - under_y)
        curl_y = (hx - under_x) - (hz - prev_x(hz))
        curl_z = (hy - prev_x(hy)) - (hx - prev_y(hx, hsx, z))
        out[z * cx : (z + 1) * cx] = ex[:cx] + kz * (curl_x[:cx] - jx)
        out[(NZ + z) * cx : (NZ + z + 1) * cx] = ey[:cx] + kz * (curl_y[:cx] - jy)
        out[(2 * NZ + z) * cx : (2 * NZ + z + 1) * cx] = kz * curl_z[:cx]
        under_x, under_y = hx, hy
        ex, ey = above_x, above_y


def shift(value, axis, steps):
    count = lax.axis_size(axis)
    return lax.ppermute(value, axis, [(i, (i + steps) % count) for i in range(count)])


def gather(value, axis):
    return [value] + [shift(value, axis, s) for s in range(1, lax.axis_size(axis))]


def per_device(e_field, h_field, inverse_permittivity, monitor_layer, source_layer, residual_far):
    cx, cy = e_field.shape[2:]
    rows = cx + 8
    nx, ny = lax.axis_size("gx"), lax.axis_size("gy")
    dirs_x, dirs_y = residual_far.shape[3:]
    part = functools.partial
    e = e_field.reshape(3 * NZ * cx, cy)
    h = h_field.reshape(3 * NZ * cx, cy)
    k = inverse_permittivity.reshape(NZ * cx, cy)

    up, down, own = call(
        part(pack_edges, cx=cx), "pack_edges",
        [(12 * NZ + 24, cy), (9 * NZ + 24, cy), (8 * cx, LANES)],
    )(e, h, k, source_layer)
    before = shift(up, "gx", 1)
    after = shift(down, "gx", -1)

    pieces = call(
        part(spread_x, cx=cx, dirs_x=dirs_x, dirs_y=dirs_y, count=nx), "spread_x",
        [(4 * cx + 8, 2 * dirs_y)] * nx,
    )(residual_far)
    far_table, source_table = call(
        part(tables, cy=cy, dirs=dirs_y, count=ny), "tables",
        [(ny * cy, 4 * dirs_y), (ny * 4 * dirs_y, cy + LANES)],
    )()

    up, down, ext = call(
        part(pack_strips, cx=cx), "pack_strips",
        [(2 * rows, LANES), (2 * rows, LANES), (8 * rows, LANES)],
    )(own, before, after)
    left = shift(up, "gy", 1)
    right = shift(down, "gy", -1)

    mixed = pieces[0]
    for s in range(1, nx):
        mixed = mixed + shift(pieces[s], "gx", s)

    e_forward, planes, kext, kstrip, lext, lstrip = call(
        part(forward, cx=cx), "forward",
        [(3 * NZ * cx, cy), (4 * cx, cy), (NZ * rows, cy), (rows, LANES), (rows, cy), (rows, LANES)],
        [pltpu.VMEM((3 * NZ * rows, cy), F32), pltpu.VMEM((3 * NZ * rows, cy), F32)],
    )(e, h, k, source_layer, monitor_layer, before, after, ext, left, right)

    spectrum = call(
        part(project_y, cx=cx, cy=cy, dirs=dirs_y, count=ny), "project_y", (4 * cx, 2 * dirs_y)
    )(*gather(planes, "gy"), far_table)
    scale = 1.0 / math.sqrt(cx * nx * cy * ny)
    far_field = call(
        part(project_x, cx=cx, dirs_x=dirs_x, dirs_y=dirs_y, count=nx, scale=scale), "project_x",
        residual_far.shape,
    )(*gather(spectrum, "gx"))

    e_adjoint = call(
        part(adjoint, cx=cx, cy=cy, dirs=dirs_y, count=ny), "adjoint", (3 * NZ * cx, cy)
    )(*gather(mixed, "gy"), source_table, kext, kstrip, lext, lstrip)
    return (e_forward.reshape(e_field.shape), far_field, e_adjoint.reshape(e_field.shape))


def solution(mesh):
    in_specs = (
        P("design", None, "gx", "gy"),
        P("design", None, "gx", "gy"),
        P("design", "gx", "gy"),
        P(("design", "gx"), "gy"),
        P(("design", "gx"), "gy"),
        P("design", None, None, "gx", "gy"),
    )
    out_specs = (
        P("design", None, "gx", "gy"),
        P("design", None, None, "gx", "gy"),
        P("design", None, "gx", "gy"),
    )
    return jax.shard_map(
        per_device, mesh=mesh, in_specs=in_specs, out_specs=out_specs, check_vma=False
    )
```

time: 231 us -> 49.1 us (0.21)
  local copies, waits for them, and re-layouts: 71.8 us -> 3.72 us
  waiting for transfers between devices: 50.9 us -> 2.15 us
  blocking collectives: 25.9 us -> 0 us
  Pallas kernels: 0 us -> 21.2 us
  starting transfers between devices: 39.6 us -> 20.9 us
  other arithmetic: 17.8 us -> 0.01 us
  between operations: 15.1 us -> 0.76 us
  matrix products: 8.32 us -> 0 us
    unnamed x5 -> x0, waiting for transfers between devices: 40.1 us -> none
    unnamed x142 -> x32, local copies, waits for them, and re-layouts: 30 us -> 3.72 us
    all_gather x1 -> x0, blocking collectives: 25.9 us -> none  [per_device(): piece = lax.all_gather(residual_far, 'gy', axis=4, tiled=True)]
    pallas_call x0 -> x8, Pallas kernels: none -> 21.2 us  [the longest x1 4.77 us: per_device(): call(part(forward, cx=cx), 'forward', [(3 * NZ * cx, cy), (4 * cx, cy), (...]
    slice x48 -> x0, local copies, waits for them, and re-layouts: 18.6 us -> none  [the longest x4 1.82 us: step_electric(): magn[2][:, -1:, :]]
    ppermute x16, starting transfers between devices: 39.4 us -> 20.9 us  [shift(): lax.ppermute(value, axis, [(i, (i + steps) % count) for i in range(count)])]
    squeeze x19 -> x0, local copies, waits for them, and re-layouts: 9.13 us -> none  [the longest x4 4.06 us: step_magnetic(): next_x2 = jnp.concatenate([elec[2][:, 1:, :], face_x[1]], axis=1)]
    another operation x26 -> x0, other arithmetic: 8.99 us -> none  [the longest x5 5.85 us: step_magnetic(): return magn - courant * jnp.stack([curl_x, curl_y, curl_z])]
  transfers between devices with their start and end apart: 19 -> 16, of which waited for: 5 -> 1; matrix products, arithmetic and copies ran while one was open for 26% -> 0% of each run, Pallas kernels for 0% -> 35%
where the time goes in v1:
time: 49.1 us; the launch traced here: 48.7 us
  Pallas kernels  21.2 us (43%)
  starting transfers between devices  20.9 us (43%)
  local copies, waits for them, and re-layouts  3.72 us (8%)
  waiting for transfers between devices  2.15 us (4%)
  between operations  0.76 us (2%)
    ppermute x16, starting transfers between devices, shift(): lax.ppermute(value, axis, [(i, (i + steps) % count) for i in range(count)])  20.9 us
    pallas_call x1, Pallas kernels, per_device(): call(part(forward, cx=cx), 'forward', [(3 * NZ * cx, cy), (4 * cx, cy), (...  4.77 us
    unnamed x32, local copies, waits for them, and re-layouts  3.72 us
    pallas_call x1, Pallas kernels, per_device(): call(part(adjoint, cx=cx, cy=cy, dirs=dirs_y, count=ny), 'adjoint', (3 *...  3.35 us
    pallas_call x1, Pallas kernels, per_device(): call(part(tables, cy=cy, dirs=dirs_y, count=ny), 'tables', [(ny * cy, 4 *...  2.83 us
    pallas_call x1, Pallas kernels, per_device(): call(part(pack_edges, cx=cx), 'pack_edges', [(12 * NZ + 24, cy), (9 * NZ...  2.26 us
    pallas_call x1, Pallas kernels, per_device(): call(part(project_y, cx=cx, cy=cy, dirs=dirs_y, count=ny), 'project_y', (...  2.18 us
    ppermute x16, waiting for transfers between devices, shift(): lax.ppermute(value, axis, [(i, (i + steps) % count) for i in range(count)])  2.15 us
  transfers between devices with their start and end apart: 16, of which 1 were waited for; matrix products, arithmetic and copies ran while one was open for 0% of the time, Pallas kernels for 35%

profile of v1, /device:TPU:0, one launch (start us, length us, event | category | flops | bytes accessed | tf_op | source)
XLA Modules:
  0.0 48.7 jit_solution(1330852561757223020)
XLA Ops:
  0.6 2.3 %pack_edges.1 = (f32[216,128]{1,0:T(8,128)}, f32[168,128]{1,0:T(8,128)}, f32[128,128]{1,0:T(8,128)}) custom-call(f32[768,128]{1,0:T(8,128)} %bitcast.5, f32[768,128]{1,0:T(8,128)} %bitcast.7, f32[256,128]{1,0:T(8,128)} %bitcast.9, s32[16,128]{1,0:T(8,128)} %layer.3), custom_call_target="tpu_custom_call" | custom-call | tf_op jit(solution)/shard_map/pack_edges/pallas_call | solution.py:471
  3.4 1.9 %collective-permute-start.1 = (f32[168,128]{1,0:T(8,128)}, f32[168,128]{1,0:T(8,128)S(1)}, u32[]{:S(2)}, u32[]{:S(2)}) collective-permute-start(f32[168,128]{1,0:T(8,128)} %get-tuple-element.22), channel_id=1, source_target_pairs={{0,12},{4,0},{8,4},{12,8},{1,13},{5,1},{9,5},{13,9},{2,14},{6,2},{... | collective-permute-start | bytes 258056 | tf_op jit(solution)/shard_map/ppermute | solution.py:454
  5.3 2.1 %spread_x.1 = (f32[72,128]{1,0:T(8,128)}, f32[72,128]{1,0:T(8,128)}, f32[72,128]{1,0:T(8,128)}, f32[72,128]{1,0:T(8,128)}) custom-call(f32[2,2,2,64,64]{4,3,2,1,0:T(8,128)} %residual.1), custom_call_target="tpu_custom_call" | custom-call | tf_op jit(solution)/shard_map/spread_x/pallas_call | solution.py:478
  7.4 0.7 %collective-permute-start.12 = (f32[72,128]{1,0:T(8,128)}, f32[72,128]{1,0:T(8,128)S(1)}, u32[]{:S(2)}, u32[]{:S(2)}) collective-permute-start(f32[72,128]{1,0:T(8,128)} %get-tuple-element.33), channel_id=1, source_target_pairs={{0,12},{4,0},{8,4},{12,8},{1,13},{5,1},{9,5},{13,9},{2,14},{6,2},{... | collective-permute-start | bytes 110600 | tf_op jit(solution)/shard_map/ppermute | solution.py:454
  8.1 1.6 %collective-permute-start.11 = (f32[72,128]{1,0:T(8,128)}, f32[72,128]{1,0:T(8,128)S(1)}, u32[]{:S(2)}, u32[]{:S(2)}) collective-permute-start(f32[72,128]{1,0:T(8,128)} %get-tuple-element.32), channel_id=1, source_target_pairs={{0,8},{4,12},{8,0},{12,4},{1,9},{5,13},{9,1},{13,5},{2,10},{6,14},... | collective-permute-start | bytes 110600 | tf_op jit(solution)/shard_map/ppermute | solution.py:454
  10.0 0.6 %copy-done.1 = f32[168,128]{1,0:T(8,128)} copy-done((f32[168,128]{1,0:T(8,128)}, f32[168,128]{1,0:T(8,128)S(1)}, u32[]{:S(2)}) %copy-start.1) | copy-done | bytes 86040
  10.6 1.7 %pack_strips.1 = (f32[48,128]{1,0:T(8,128)}, f32[48,128]{1,0:T(8,128)}, f32[192,128]{1,0:T(8,128)}) custom-call(f32[128,128]{1,0:T(8,128)} %get-tuple-element.23.own, f32[216,128]{1,0:T(8,128)} %copy-done, f32[168,128]{1,0:T(8,128)} %copy-done.1), custom_call_target="tpu_custom_call" | custom-call | tf_op jit(solution)/shard_map/pack_strips/pallas_call | solution.py:487
  12.4 1.6 %collective-permute-start.2 = (f32[48,128]{1,0:T(8,128)}, f32[48,128]{1,0:T(8,128)S(1)}, u32[]{:S(2)}, u32[]{:S(2)}) collective-permute-start(f32[48,128]{1,0:T(8,128)} %get-tuple-element.25), channel_id=1, source_target_pairs={{0,1},{1,2},{2,3},{3,0},{4,5},{5,6},{6,7},{7,4},{8,9},{9,10},{10,1... | collective-permute-start | bytes 73736 | tf_op jit(solution)/shard_map/ppermute | solution.py:454
  13.9 2.2 %collective-permute-start.3 = (f32[48,128]{1,0:T(8,128)}, f32[48,128]{1,0:T(8,128)S(1)}, u32[]{:S(2)}, u32[]{:S(2)}) collective-permute-start(f32[48,128]{1,0:T(8,128)} %get-tuple-element.26), channel_id=1, source_target_pairs={{0,3},{1,0},{2,1},{3,2},{4,7},{5,4},{6,5},{7,6},{8,11},{9,8},{10,9... | collective-permute-start | bytes 73736 | tf_op jit(solution)/shard_map/ppermute | solution.py:454
  16.2 2.1 %collective-permute-done.2.left = f32[48,128]{1,0:T(8,128)S(1)} collective-permute-done((f32[48,128]{1,0:T(8,128)}, f32[48,128]{1,0:T(8,128)S(1)}, u32[]{:S(2)}, u32[]{:S(2)}) %collective-permute-start.2) | collective-permute-done | bytes 24608 | tf_op jit(solution)/shard_map/ppermute | solution.py:454
  18.3 0.6 %copy-done.14 = f32[48,128]{1,0:T(8,128)} copy-done((f32[48,128]{1,0:T(8,128)}, f32[48,128]{1,0:T(8,128)S(1)}, u32[]{:S(2)}) %copy-start.14) | copy-done | bytes 24600
  18.9 4.8 %forward.1 = (f32[768,128]{1,0:T(8,128)}, f32[64,128]{1,0:T(8,128)}, f32[384,128]{1,0:T(8,128)}, f32[24,128]{1,0:T(8,128)}, f32[24,128]{1,0:T(8,128)}, /*index=5*/f32[24,128]{1,0:T(8,128)}) custom-call(f32[768,128]{1,0:T(8,128)} %bitcast.6, f32[768,128]{1,0:T(8,128)} %bitcast.8, f32[256,128]{1,0:T(8,128)} %bitcast.10, s32[16,128]{1,0:T(8,128)} %layer.3, ...), custom_call_target="tpu_custom_call" | custom-call | tf_op jit(solution)/shard_map/forward/pallas_call | solution.py:498
  23.7 1.3 %collective-permute-start.4 = (f32[64,128]{1,0:T(8,128)}, f32[64,128]{1,0:T(8,128)S(1)}, u32[]{:S(2)}, u32[]{:S(2)}) collective-permute-start(f32[64,128]{1,0:T(8,128)} %get-tuple-element.28.refs_0_), channel_id=1, source_target_pairs={{0,1},{1,2},{2,3},{3,0},{4,5},{5,6},{6,7},{7,4},{8,9},{9,10},{10,1... | collective-permute-start | bytes 98312 | tf_op jit(solution)/shard_map/ppermute | solution.py:454
  25.0 1.6 %collective-permute-start.13 = (f32[72,128]{1,0:T(8,128)S(1)}, f32[72,128]{1,0:T(8,128)S(1)}, u32[]{:S(2)}, u32[]{:S(2)}) collective-permute-start(f32[72,128]{1,0:T(8,128)S(1)} %add_add_fusion.refs_0_), channel_id=1, source_target_pairs={{0,1},{1,2},{2,3},{3,0},{4,5},{5,6},{6,7},{7,4},{8,9},{9,10},{10,1... | collective-permute-start | bytes 110600 | tf_op jit(solution)/shard_map/ppermute | solution.py:454
  26.7 2.1 %collective-permute-start.5 = (f32[64,128]{1,0:T(8,128)S(1)}, f32[64,128]{1,0:T(8,128)S(1)}, u32[]{:S(2)}, u32[]{:S(2)}) collective-permute-start(f32[64,128]{1,0:T(8,128)S(1)} %copy-done.10), channel_id=1, source_target_pairs={{0,2},{1,3},{2,0},{3,1},{4,6},{5,7},{6,4},{7,5},{8,10},{9,11},{10,... | collective-permute-start | bytes 98312 | tf_op jit(solution)/shard_map/ppermute | solution.py:454
  28.8 2.2 %collective-permute-start.6 = (f32[64,128]{1,0:T(8,128)S(1)}, f32[64,128]{1,0:T(8,128)S(1)}, u32[]{:S(2)}, u32[]{:S(2)}) collective-permute-start(f32[64,128]{1,0:T(8,128)S(1)} %copy-done.10), channel_id=1, source_target_pairs={{0,3},{1,0},{2,1},{3,2},{4,7},{5,4},{6,5},{7,6},{8,11},{9,8},{10,9... | collective-permute-start | bytes 98312 | tf_op jit(solution)/shard_map/ppermute | solution.py:454
  31.1 2.1 %collective-permute-start.15 = (f32[72,128]{1,0:T(8,128)S(1)}, f32[72,128]{1,0:T(8,128)S(1)}, u32[]{:S(2)}, u32[]{:S(2)}) collective-permute-start(f32[72,128]{1,0:T(8,128)S(1)} %add_add_fusion.refs_0_), channel_id=1, source_target_pairs={{0,3},{1,0},{2,1},{3,2},{4,7},{5,4},{6,5},{7,6},{8,11},{9,8},{10,9... | collective-permute-start | bytes 110600 | tf_op jit(solution)/shard_map/ppermute | solution.py:454
  33.2 2.8 %tables.1 = (f32[512,256]{1,0:T(8,128)}, f32[1024,256]{1,0:T(8,128)}) custom-call(), custom_call_target="tpu_custom_call" | custom-call | tf_op jit(solution)/shard_map/tables/pallas_call | solution.py:482
  36.6 2.2 %project_y.1.refs_0_ = f32[64,128]{1,0:T(8,128)} custom-call(f32[64,128]{1,0:T(8,128)} %get-tuple-element.28.refs_0_, f32[64,128]{1,0:T(8,128)} %copy-done.11, f32[64,128]{1,0:T(8,128)} %copy-done.12, f32[64,128]{1,0:T(8,128)} %copy-done.13, f32[512,256]{1,0:T(8,128)} %get-tuple-element.29.refs_4_), custom_call_target="tpu_custom_call" | custom-call | tf_op jit(solution)/shard_map/project_y/pallas_call | solution.py:504
  38.8 1.2 %collective-permute-start.8 = (f32[64,128]{1,0:T(8,128)}, f32[64,128]{1,0:T(8,128)S(1)}, u32[]{:S(2)}, u32[]{:S(2)}) collective-permute-start(f32[64,128]{1,0:T(8,128)} %project_y.1.refs_0_), channel_id=1, source_target_pairs={{0,8},{4,12},{8,0},{12,4},{1,9},{5,13},{9,1},{13,5},{2,10},{6,14},... | collective-permute-start | bytes 98312 | tf_op jit(solution)/shard_map/ppermute | solution.py:454
  40.0 1.5 %collective-permute-start.9 = (f32[64,128]{1,0:T(8,128)}, f32[64,128]{1,0:T(8,128)S(1)}, u32[]{:S(2)}, u32[]{:S(2)}) collective-permute-start(f32[64,128]{1,0:T(8,128)} %project_y.1.refs_0_), channel_id=1, source_target_pairs={{0,12},{4,0},{8,4},{12,8},{1,13},{5,1},{9,5},{13,9},{2,14},{6,2},{... | collective-permute-start | bytes 98312 | tf_op jit(solution)/shard_map/ppermute | solution.py:454
  42.1 3.4 %adjoint.1 = f32[768,128]{1,0:T(8,128)} custom-call(f32[72,128]{1,0:T(8,128)} %copy-done.2, f32[72,128]{1,0:T(8,128)} %copy-done.4, f32[72,128]{1,0:T(8,128)} %copy-done.5, f32[72,128]{1,0:T(8,128)} %copy-done.6, f32[1024,256]{1,0:T(8,128)} %get-tuple-element.34.refs_4_, f32[384,128]{1,0:T(8,128)} %get-tuple-element.35.refs_5_, ...), custom_call_target="tpu_custom_call" | custom-call | tf_op jit(solution)/shard_map/adjoint/pallas_call | solution.py:513
  46.1 0.6 %copy-done.9 = f32[64,128]{1,0:T(8,128)} copy-done((f32[64,128]{1,0:T(8,128)}, f32[64,128]{1,0:T(8,128)S(1)}, u32[]{:S(2)}) %copy-start.9) | copy-done | bytes 32792
  46.7 2.0 %project_x.1 = f32[2,2,2,64,64]{4,3,2,1,0:T(8,128)} custom-call(f32[64,128]{1,0:T(8,128)} %project_y.1.refs_0_, f32[64,128]{1,0:T(8,128)} %copy-done.7, f32[64,128]{1,0:T(8,128)} %copy-done.8, f32[64,128]{1,0:T(8,128)} %copy-done.9), custom_call_target="tpu_custom_call" | custom-call | tf_op jit(solution)/shard_map/project_x/pallas_call | solution.py:508
  (49 shorter events, 2.7 us)
Async XLA Ops:
  2.9 7.1 %collective-permute-start = (f32[216,128]{1,0:T(8,128)}, f32[216,128]{1,0:T(8,128)S(1)}, u32[]{:S(2)}, u32[]{:S(2)}) collective-permute-start(f32[216,128]{1,0:T(8,128)} %get-tuple-element.21), channel_id=1, source_target_pairs={{0,4},{4,8},{8,12},{12,0},{1,5},{5,9},{9,13},{13,1},{2,6},{6,10},{... | collective-permute-start | bytes 331784 | tf_op jit(solution)/shard_map/ppermute | solution.py:454
  3.4 6.6 %collective-permute-start.1 = (f32[168,128]{1,0:T(8,128)}, f32[168,128]{1,0:T(8,128)S(1)}, u32[]{:S(2)}, u32[]{:S(2)}) collective-permute-start(f32[168,128]{1,0:T(8,128)} %get-tuple-element.22), channel_id=1, source_target_pairs={{0,12},{4,0},{8,4},{12,8},{1,13},{5,1},{9,5},{13,9},{2,14},{6,2},{... | collective-permute-start | bytes 258056 | tf_op jit(solution)/shard_map/ppermute | solution.py:454
  7.4 17.5 %collective-permute-start.12 = (f32[72,128]{1,0:T(8,128)}, f32[72,128]{1,0:T(8,128)S(1)}, u32[]{:S(2)}, u32[]{:S(2)}) collective-permute-start(f32[72,128]{1,0:T(8,128)} %get-tuple-element.33), channel_id=1, source_target_pairs={{0,12},{4,0},{8,4},{12,8},{1,13},{5,1},{9,5},{13,9},{2,14},{6,2},{... | collective-permute-start | bytes 110600 | tf_op jit(solution)/shard_map/ppermute | solution.py:454
  8.1 16.9 %collective-permute-start.11 = (f32[72,128]{1,0:T(8,128)}, f32[72,128]{1,0:T(8,128)S(1)}, u32[]{:S(2)}, u32[]{:S(2)}) collective-permute-start(f32[72,128]{1,0:T(8,128)} %get-tuple-element.32), channel_id=1, source_target_pairs={{0,8},{4,12},{8,0},{12,4},{1,9},{5,13},{9,1},{13,5},{2,10},{6,14},... | collective-permute-start | bytes 110600 | tf_op jit(solution)/shard_map/ppermute | solution.py:454
  9.7 15.2 %collective-permute-start.10 = (f32[72,128]{1,0:T(8,128)}, f32[72,128]{1,0:T(8,128)S(1)}, u32[]{:S(2)}, u32[]{:S(2)}) collective-permute-start(f32[72,128]{1,0:T(8,128)} %get-tuple-element.31), channel_id=1, source_target_pairs={{0,4},{4,8},{8,12},{12,0},{1,5},{5,9},{9,13},{13,1},{2,6},{6,10},{... | collective-permute-start | bytes 110600 | tf_op jit(solution)/shard_map/ppermute | solution.py:454
  10.0 0.6 %copy-start.1 = (f32[168,128]{1,0:T(8,128)}, f32[168,128]{1,0:T(8,128)S(1)}, u32[]{:S(2)}) copy-start(f32[168,128]{1,0:T(8,128)S(1)} %collective-permute-done.1.after) | copy-start | bytes 258052
  10.0 0.7 %copy-start = (f32[216,128]{1,0:T(8,128)}, f32[216,128]{1,0:T(8,128)S(1)}, u32[]{:S(2)}) copy-start(f32[216,128]{1,0:T(8,128)S(1)} %collective-permute-done.before) | copy-start | bytes 331780
  12.4 5.9 %collective-permute-start.2 = (f32[48,128]{1,0:T(8,128)}, f32[48,128]{1,0:T(8,128)S(1)}, u32[]{:S(2)}, u32[]{:S(2)}) collective-permute-start(f32[48,128]{1,0:T(8,128)} %get-tuple-element.25), channel_id=1, source_target_pairs={{0,1},{1,2},{2,3},{3,0},{4,5},{5,6},{6,7},{7,4},{8,9},{9,10},{10,1... | collective-permute-start | bytes 73736 | tf_op jit(solution)/shard_map/ppermute | solution.py:454
  13.9 4.4 %collective-permute-start.3 = (f32[48,128]{1,0:T(8,128)}, f32[48,128]{1,0:T(8,128)S(1)}, u32[]{:S(2)}, u32[]{:S(2)}) collective-permute-start(f32[48,128]{1,0:T(8,128)} %get-tuple-element.26), channel_id=1, source_target_pairs={{0,3},{1,0},{2,1},{3,2},{4,7},{5,4},{6,5},{7,6},{8,11},{9,8},{10,9... | collective-permute-start | bytes 73736 | tf_op jit(solution)/shard_map/ppermute | solution.py:454
  18.3 0.6 %copy-start.15 = (f32[48,128]{1,0:T(8,128)}, f32[48,128]{1,0:T(8,128)S(1)}, u32[]{:S(2)}) copy-start(f32[48,128]{1,0:T(8,128)S(1)} %collective-permute-done.3.right) | copy-start | bytes 73732
  18.9 6.1 %copy-start.3 = (f32[72,128]{1,0:T(8,128)S(1)}, f32[72,128]{1,0:T(8,128)}, u32[]{:S(2)}) copy-start(f32[72,128]{1,0:T(8,128)} %get-tuple-element.30) | copy-start | bytes 110596
  23.7 7.3 %collective-permute-start.4 = (f32[64,128]{1,0:T(8,128)}, f32[64,128]{1,0:T(8,128)S(1)}, u32[]{:S(2)}, u32[]{:S(2)}) collective-permute-start(f32[64,128]{1,0:T(8,128)} %get-tuple-element.28.refs_0_), channel_id=1, source_target_pairs={{0,1},{1,2},{2,3},{3,0},{4,5},{5,6},{6,7},{7,4},{8,9},{9,10},{10,1... | collective-permute-start | bytes 98312 | tf_op jit(solution)/shard_map/ppermute | solution.py:454
  25.0 1.7 %copy-start.10 = (f32[64,128]{1,0:T(8,128)S(1)}, f32[64,128]{1,0:T(8,128)}, u32[]{:S(2)}) copy-start(f32[64,128]{1,0:T(8,128)} %get-tuple-element.28.refs_0_) | copy-start | bytes 98308
  25.0 13.8 %copy-start.2 = (f32[72,128]{1,0:T(8,128)}, f32[72,128]{1,0:T(8,128)S(1)}, u32[]{:S(2)}) copy-start(f32[72,128]{1,0:T(8,128)S(1)} %add_add_fusion.refs_0_) | copy-start | bytes 110596
  25.0 15.0 %collective-permute-start.13 = (f32[72,128]{1,0:T(8,128)S(1)}, f32[72,128]{1,0:T(8,128)S(1)}, u32[]{:S(2)}, u32[]{:S(2)}) collective-permute-start(f32[72,128]{1,0:T(8,128)S(1)} %add_add_fusion.refs_0_), channel_id=1, source_target_pairs={{0,1},{1,2},{2,3},{3,0},{4,5},{5,6},{6,7},{7,4},{8,9},{9,10},{10,1... | collective-permute-start | bytes 110600 | tf_op jit(solution)/shard_map/ppermute | solution.py:454
  26.7 9.4 %collective-permute-start.5 = (f32[64,128]{1,0:T(8,128)S(1)}, f32[64,128]{1,0:T(8,128)S(1)}, u32[]{:S(2)}, u32[]{:S(2)}) collective-permute-start(f32[64,128]{1,0:T(8,128)S(1)} %copy-done.10), channel_id=1, source_target_pairs={{0,2},{1,3},{2,0},{3,1},{4,6},{5,7},{6,4},{7,5},{8,10},{9,11},{10,... | collective-permute-start | bytes 98312 | tf_op jit(solution)/shard_map/ppermute | solution.py:454
  28.8 7.2 %collective-permute-start.6 = (f32[64,128]{1,0:T(8,128)S(1)}, f32[64,128]{1,0:T(8,128)S(1)}, u32[]{:S(2)}, u32[]{:S(2)}) collective-permute-start(f32[64,128]{1,0:T(8,128)S(1)} %copy-done.10), channel_id=1, source_target_pairs={{0,3},{1,0},{2,1},{3,2},{4,7},{5,4},{6,5},{7,6},{8,11},{9,8},{10,9... | collective-permute-start | bytes 98312 | tf_op jit(solution)/shard_map/ppermute | solution.py:454
  31.0 10.5 %collective-permute-start.14 = (f32[72,128]{1,0:T(8,128)S(1)}, f32[72,128]{1,0:T(8,128)S(1)}, u32[]{:S(2)}, u32[]{:S(2)}) collective-permute-start(f32[72,128]{1,0:T(8,128)S(1)} %add_add_fusion.refs_0_), channel_id=1, source_target_pairs={{0,2},{1,3},{2,0},{3,1},{4,6},{5,7},{6,4},{7,5},{8,10},{9,11},{10,... | collective-permute-start | bytes 110600 | tf_op jit(solution)/shard_map/ppermute | solution.py:454
  31.1 5.0 %copy-start.11 = (f32[64,128]{1,0:T(8,128)}, f32[64,128]{1,0:T(8,128)S(1)}, u32[]{:S(2)}) copy-start(f32[64,128]{1,0:T(8,128)S(1)} %collective-permute-done.4.refs_1_) | copy-start | bytes 98308
  31.1 10.4 %collective-permute-start.15 = (f32[72,128]{1,0:T(8,128)S(1)}, f32[72,128]{1,0:T(8,128)S(1)}, u32[]{:S(2)}, u32[]{:S(2)}) collective-permute-start(f32[72,128]{1,0:T(8,128)S(1)} %add_add_fusion.refs_0_), channel_id=1, source_target_pairs={{0,3},{1,0},{2,1},{3,2},{4,7},{5,4},{6,5},{7,6},{8,11},{9,8},{10,9... | collective-permute-start | bytes 110600 | tf_op jit(solution)/shard_map/ppermute | solution.py:454
  38.8 6.7 %collective-permute-start.7 = (f32[64,128]{1,0:T(8,128)}, f32[64,128]{1,0:T(8,128)S(1)}, u32[]{:S(2)}, u32[]{:S(2)}) collective-permute-start(f32[64,128]{1,0:T(8,128)} %project_y.1.refs_0_), channel_id=1, source_target_pairs={{0,4},{4,8},{8,12},{12,0},{1,5},{5,9},{9,13},{13,1},{2,6},{6,10},{... | collective-permute-start | bytes 98312 | tf_op jit(solution)/shard_map/ppermute | solution.py:454
  38.8 6.7 %collective-permute-start.8 = (f32[64,128]{1,0:T(8,128)}, f32[64,128]{1,0:T(8,128)S(1)}, u32[]{:S(2)}, u32[]{:S(2)}) collective-permute-start(f32[64,128]{1,0:T(8,128)} %project_y.1.refs_0_), channel_id=1, source_target_pairs={{0,8},{4,12},{8,0},{12,4},{1,9},{5,13},{9,1},{13,5},{2,10},{6,14},... | collective-permute-start | bytes 98312 | tf_op jit(solution)/shard_map/ppermute | solution.py:454
  40.0 1.5 %copy-start.4 = (f32[72,128]{1,0:T(8,128)}, f32[72,128]{1,0:T(8,128)S(1)}, u32[]{:S(2)}) copy-start(f32[72,128]{1,0:T(8,128)S(1)} %collective-permute-done.13.refs_1_) | copy-start | bytes 110596
  40.0 5.5 %collective-permute-start.9 = (f32[64,128]{1,0:T(8,128)}, f32[64,128]{1,0:T(8,128)S(1)}, u32[]{:S(2)}, u32[]{:S(2)}) collective-permute-start(f32[64,128]{1,0:T(8,128)} %project_y.1.refs_0_), channel_id=1, source_target_pairs={{0,12},{4,0},{8,4},{12,8},{1,13},{5,1},{9,5},{13,9},{2,14},{6,2},{... | collective-permute-start | bytes 98312 | tf_op jit(solution)/shard_map/ppermute | solution.py:454
  (8 other events, 4.9 us)

commit v2 on v1

--- a/solution.py
+++ b/solution.py
@@ -45,15 +45,28 @@
     return jnp.concatenate([value[:, half:], value[:, :half]], axis=1)
 
 
-def call(kernel, name, out, scratch=()):
+def call(kernel, name, out, scratch=(), far=(), far_out=()):
     single = isinstance(out[0], int)
-    shapes = [jax.ShapeDtypeStruct(s, F32) for s in ([out] if single else out)]
-    return pl.pallas_call(
-        kernel,
-        out_shape=shapes[0] if single else tuple(shapes),
-        scratch_shapes=list(scratch),
-        name=name,
-    )
+    near = pl.BlockSpec(memory_space=pltpu.VMEM)
+    shapes = []
+    for i, shape in enumerate([out] if single else out):
+        shapes.append(jax.ShapeDtypeStruct(shape, F32) if i in far_out else pltpu.VMEM(shape, F32))
+
+    def run(*args):
+        args = [
+            x if i in far else pltpu.with_memory_space_constraint(x, pltpu.VMEM)
+            for i, x in enumerate(args)
+        ]
+        return pl.pallas_call(
+            kernel,
+            out_shape=shapes[0] if single else tuple(shapes),
+            in_specs=[near] * len(args),
+            out_specs=near if single else tuple([near] * len(shapes)),
+            scratch_shapes=list(scratch),
+            name=name,
+        )(*args)
+
+    return run
 
 
 def pack_edges(e, h, k, layer, up, down, own, *, cx):
@@ -470,14 +483,14 @@
 
     up, down, own = call(
         part(pack_edges, cx=cx), "pack_edges",
-        [(12 * NZ + 24, cy), (9 * NZ + 24, cy), (8 * cx, LANES)],
+        [(12 * NZ + 24, cy), (9 * NZ + 24, cy), (8 * cx, LANES)], far=(0, 1, 2, 3),
     )(e, h, k, source_layer)
     before = shift(up, "gx", 1)
     after = shift(down, "gx", -1)
 
     pieces = call(
         part(spread_x, cx=cx, dirs_x=dirs_x, dirs_y=dirs_y, count=nx), "spread_x",
-        [(4 * cx + 8, 2 * dirs_y)] * nx,
+        [(4 * cx + 8, 2 * dirs_y)] * nx, far=(0,),
     )(residual_far)
     far_table, source_table = call(
         part(tables, cy=cy, dirs=dirs_y, count=ny), "tables",
@@ -499,6 +512,7 @@
         part(forward, cx=cx), "forward",
         [(3 * NZ * cx, cy), (4 * cx, cy), (NZ * rows, cy), (rows, LANES), (rows, cy), (rows, LANES)],
         [pltpu.VMEM((3 * NZ * rows, cy), F32), pltpu.VMEM((3 * NZ * rows, cy), F32)],
+        far=(0, 1, 2, 3, 4), far_out=(0,),
     )(e, h, k, source_layer, monitor_layer, before, after, ext, left, right)
 
     spectrum = call(
@@ -507,11 +521,11 @@
     scale = 1.0 / math.sqrt(cx * nx * cy * ny)
     far_field = call(
         part(project_x, cx=cx, dirs_x=dirs_x, dirs_y=dirs_y, count=nx, scale=scale), "project_x",
-        residual_far.shape,
+        residual_far.shape, far_out=(0,),
     )(*gather(spectrum, "gx"))
 
     e_adjoint = call(
-        part(adjoint, cx=cx, cy=cy, dirs=dirs_y, count=ny), "adjoint", (3 * NZ * cx, cy)
+        part(adjoint, cx=cx, cy=cy, dirs=dirs_y, count=ny), "adjoint", (3 * NZ * cx, cy), far_out=(0,)
     )(*gather(mixed, "gy"), source_table, kext, kstrip, lext, lstrip)
     return (e_forward.reshape(e_field.shape), far_field, e_adjoint.reshape(e_field.shape))
 

time: 49.1 us -> 36.9 us (0.75)
  Pallas kernels: 21.2 us -> 13.1 us
  local copies, waits for them, and re-layouts: 3.72 us -> 0 us
    pallas_call x8, Pallas kernels: 21.2 us -> 13.1 us  [run(): pl.pallas_call(kernel, out_shape=shapes[0] if single else tuple(shapes),...]
    unnamed x32 -> x0, local copies, waits for them, and re-layouts: 3.72 us -> none
  transfers between devices with their start and end apart: 16 -> 16, of which waited for: 1 -> 2; matrix products, arithmetic and copies ran while one was open for 0% -> 0% of each run, Pallas kernels for 35% -> 28%
where the time goes in v2:
time: 36.9 us; the launch traced here: 36.7 us
  starting transfers between devices  20.8 us (56%)
  Pallas kernels  13.1 us (36%)
  waiting for transfers between devices  2.01 us (5%)
  between operations  0.71 us (2%)
    ppermute x16, starting transfers between devices, shift(): lax.ppermute(value, axis, [(i, (i + steps) % count) for i in range(count)])  20.8 us
    pallas_call x8, Pallas kernels, run(): pl.pallas_call(kernel, out_shape=shapes[0] if single else tuple(shapes),...  13.1 us
    ppermute x16, waiting for transfers between devices, shift(): lax.ppermute(value, axis, [(i, (i + steps) % count) for i in range(count)])  2.01 us
  transfers between devices with their start and end apart: 16, of which 2 were waited for; matrix products, arithmetic and copies ran while one was open for 0% of the time, Pallas kernels for 28%

profile of v2, /device:TPU:0, one launch (start us, length us, event | category | flops | bytes accessed | tf_op | source)
XLA Modules:
  0.0 36.7 jit_solution(2848545045562695461)
XLA Ops:
  0.6 1.6 %pack_edges.1 = (f32[216,128]{1,0:T(8,128)S(1)}, f32[168,128]{1,0:T(8,128)S(1)}, f32[128,128]{1,0:T(8,128)S(1)}) custom-call(f32[768,128]{1,0:T(8,128)} %bitcast.5, f32[768,128]{1,0:T(8,128)} %bitcast.7, f32[256,128]{1,0:T(8,128)} %bitcast.9, s32[16,128]{1,0:T(8,128)} %layer.3), custom_call_target="tpu_custom_call" | custom-call | tf_op jit(solution)/shard_map/pack_edges/pallas_call | solution.py:60
  2.3 0.5 %collective-permute-start = (f32[216,128]{1,0:T(8,128)S(1)}, f32[216,128]{1,0:T(8,128)S(1)}, u32[]{:S(2)}, u32[]{:S(2)}) collective-permute-start(f32[216,128]{1,0:T(8,128)S(1)} %get-tuple-element.21), channel_id=1, source_target_pairs={{0,4},{4,8},{8,12},{12,0},{1,5},{5,9},{9,13},{13,1},{2,6},{6,10},{... | collective-permute-start | bytes 331784 | tf_op jit(solution)/shard_map/ppermute | solution.py:467
  2.8 2.0 %collective-permute-start.1 = (f32[168,128]{1,0:T(8,128)S(1)}, f32[168,128]{1,0:T(8,128)S(1)}, u32[]{:S(2)}, u32[]{:S(2)}) collective-permute-start(f32[168,128]{1,0:T(8,128)S(1)} %get-tuple-element.22), channel_id=1, source_target_pairs={{0,12},{4,0},{8,4},{12,8},{1,13},{5,1},{9,5},{13,9},{2,14},{6,2},{... | collective-permute-start | bytes 258056 | tf_op jit(solution)/shard_map/ppermute | solution.py:467
  4.8 1.4 %spread_x.1 = (f32[72,128]{1,0:T(8,128)S(1)}, f32[72,128]{1,0:T(8,128)S(1)}, f32[72,128]{1,0:T(8,128)S(1)}, f32[72,128]{1,0:T(8,128)S(1)}) custom-call(f32[2,2,2,64,64]{4,3,2,1,0:T(8,128)} %residual.1), custom_call_target="tpu_custom_call" | custom-call | tf_op jit(solution)/shard_map/spread_x/pallas_call | solution.py:60
  6.3 0.7 %collective-permute-start.12 = (f32[72,128]{1,0:T(8,128)S(1)}, f32[72,128]{1,0:T(8,128)S(1)}, u32[]{:S(2)}, u32[]{:S(2)}) collective-permute-start(f32[72,128]{1,0:T(8,128)S(1)} %get-tuple-element.33), channel_id=1, source_target_pairs={{0,12},{4,0},{8,4},{12,8},{1,13},{5,1},{9,5},{13,9},{2,14},{6,2},{... | collective-permute-start | bytes 110600 | tf_op jit(solution)/shard_map/ppermute | solution.py:467
  7.0 1.6 %collective-permute-start.11 = (f32[72,128]{1,0:T(8,128)S(1)}, f32[72,128]{1,0:T(8,128)S(1)}, u32[]{:S(2)}, u32[]{:S(2)}) collective-permute-start(f32[72,128]{1,0:T(8,128)S(1)} %get-tuple-element.32), channel_id=1, source_target_pairs={{0,8},{4,12},{8,0},{12,4},{1,9},{5,13},{9,1},{13,5},{2,10},{6,14},... | collective-permute-start | bytes 110600 | tf_op jit(solution)/shard_map/ppermute | solution.py:467
  8.6 0.2 collective-permute-start.10
  8.8 0.1 pack_strips.1
  8.9 1.6 %collective-permute-start.2 = (f32[48,128]{1,0:T(8,128)S(1)}, f32[48,128]{1,0:T(8,128)S(1)}, u32[]{:S(2)}, u32[]{:S(2)}) collective-permute-start(f32[48,128]{1,0:T(8,128)S(1)} %get-tuple-element.25), channel_id=1, source_target_pairs={{0,1},{1,2},{2,3},{3,0},{4,5},{5,6},{6,7},{7,4},{8,9},{9,10},{10,1... | collective-permute-start | bytes 73736 | tf_op jit(solution)/shard_map/ppermute | solution.py:467
  10.5 2.2 %collective-permute-start.3 = (f32[48,128]{1,0:T(8,128)S(1)}, f32[48,128]{1,0:T(8,128)S(1)}, u32[]{:S(2)}, u32[]{:S(2)}) collective-permute-start(f32[48,128]{1,0:T(8,128)S(1)} %get-tuple-element.26), channel_id=1, source_target_pairs={{0,3},{1,0},{2,1},{3,2},{4,7},{5,4},{6,5},{7,6},{8,11},{9,8},{10,9... | collective-permute-start | bytes 73736 | tf_op jit(solution)/shard_map/ppermute | solution.py:467
  12.8 1.8 %collective-permute-done.2.left = f32[48,128]{1,0:T(8,128)S(1)} collective-permute-done((f32[48,128]{1,0:T(8,128)S(1)}, f32[48,128]{1,0:T(8,128)S(1)}, u32[]{:S(2)}, u32[]{:S(2)}) %collective-permute-start.2) | collective-permute-done | bytes 24608 | tf_op jit(solution)/shard_map/ppermute | solution.py:467
  14.6 0.2 collective-permute-done.3.right
  14.8 4.6 %forward.1 = (f32[768,128]{1,0:T(8,128)}, f32[64,128]{1,0:T(8,128)S(1)}, f32[384,128]{1,0:T(8,128)S(1)}, f32[24,128]{1,0:T(8,128)S(1)}, f32[24,128]{1,0:T(8,128)S(1)}, /*index=5*/f32[24,128]{1,0:T(8,128)S(1)}) custom-call(f32[768,128]{1,0:T(8,128)} %bitcast.6, f32[768,128]{1,0:T(8,128)} %bitcast.8, f32[256,128]{1,0:T(8,128)} %bitcast.10, s32[16,128]{1,0:T(8,128)} %layer.3, ...), custom_call_target="tpu_custom_call" | custom-call | tf_op jit(solution)/shard_map/forward/pallas_call | solution.py:60
  19.3 1.2 %collective-permute-start.4 = (f32[64,128]{1,0:T(8,128)S(1)}, f32[64,128]{1,0:T(8,128)S(1)}, u32[]{:S(2)}, u32[]{:S(2)}) collective-permute-start(f32[64,128]{1,0:T(8,128)S(1)} %get-tuple-element.28.refs_0_), channel_id=1, source_target_pairs={{0,1},{1,2},{2,3},{3,0},{4,5},{5,6},{6,7},{7,4},{8,9},{9,10},{10,1... | collective-permute-start | bytes 98312 | tf_op jit(solution)/shard_map/ppermute | solution.py:467
  20.5 1.6 %collective-permute-start.13 = (f32[72,128]{1,0:T(8,128)S(1)}, f32[72,128]{1,0:T(8,128)S(1)}, u32[]{:S(2)}, u32[]{:S(2)}) collective-permute-start(f32[72,128]{1,0:T(8,128)S(1)} %add_add_fusion.refs_0_), channel_id=1, source_target_pairs={{0,1},{1,2},{2,3},{3,0},{4,5},{5,6},{6,7},{7,4},{8,9},{9,10},{10,1... | collective-permute-start | bytes 110600 | tf_op jit(solution)/shard_map/ppermute | solution.py:467
  22.2 1.6 %collective-permute-start.5 = (f32[64,128]{1,0:T(8,128)S(1)}, f32[64,128]{1,0:T(8,128)S(1)}, u32[]{:S(2)}, u32[]{:S(2)}) collective-permute-start(f32[64,128]{1,0:T(8,128)S(1)} %get-tuple-element.28.refs_0_), channel_id=1, source_target_pairs={{0,2},{1,3},{2,0},{3,1},{4,6},{5,7},{6,4},{7,5},{8,10},{9,11},{10,... | collective-permute-start | bytes 98312 | tf_op jit(solution)/shard_map/ppermute | solution.py:467
  23.8 2.8 %collective-permute-start.6 = (f32[64,128]{1,0:T(8,128)S(1)}, f32[64,128]{1,0:T(8,128)S(1)}, u32[]{:S(2)}, u32[]{:S(2)}) collective-permute-start(f32[64,128]{1,0:T(8,128)S(1)} %get-tuple-element.28.refs_0_), channel_id=1, source_target_pairs={{0,3},{1,0},{2,1},{3,2},{4,7},{5,4},{6,5},{7,6},{8,11},{9,8},{10,9... | collective-permute-start | bytes 98312 | tf_op jit(solution)/shard_map/ppermute | solution.py:467
  26.5 1.6 %collective-permute-start.15 = (f32[72,128]{1,0:T(8,128)S(1)}, f32[72,128]{1,0:T(8,128)S(1)}, u32[]{:S(2)}, u32[]{:S(2)}) collective-permute-start(f32[72,128]{1,0:T(8,128)S(1)} %add_add_fusion.refs_0_), channel_id=1, source_target_pairs={{0,3},{1,0},{2,1},{3,2},{4,7},{5,4},{6,5},{7,6},{8,11},{9,8},{10,9... | collective-permute-start | bytes 110600 | tf_op jit(solution)/shard_map/ppermute | solution.py:467
  28.2 1.8 %tables.1 = (f32[512,256]{1,0:T(8,128)S(1)}, f32[1024,256]{1,0:T(8,128)S(1)}) custom-call(), custom_call_target="tpu_custom_call" | custom-call | tf_op jit(solution)/shard_map/tables/pallas_call | solution.py:60
  30.0 0.5 %project_y.1.refs_0_ = f32[64,128]{1,0:T(8,128)S(1)} custom-call(f32[64,128]{1,0:T(8,128)S(1)} %get-tuple-element.28.refs_0_, f32[64,128]{1,0:T(8,128)S(1)} %collective-permute-done.4.refs_1_, f32[64,128]{1,0:T(8,128)S(1)} %collective-permute-done.5.refs_2_, f32[64,128]{1,0:T(8,128)S(1)} %collective-permute-done.6.refs_3_, ...), custom_call_target="tpu_custom_call" | custom-call | tf_op jit(solution)/shard_map/project_y/pallas_call | solution.py:60
  30.6 1.6 %collective-permute-start.8 = (f32[64,128]{1,0:T(8,128)S(1)}, f32[64,128]{1,0:T(8,128)S(1)}, u32[]{:S(2)}, u32[]{:S(2)}) collective-permute-start(f32[64,128]{1,0:T(8,128)S(1)} %project_y.1.refs_0_), channel_id=1, source_target_pairs={{0,8},{4,12},{8,0},{12,4},{1,9},{5,13},{9,1},{13,5},{2,10},{6,14},... | collective-permute-start | bytes 98312 | tf_op jit(solution)/shard_map/ppermute | solution.py:467
  32.2 1.4 %collective-permute-start.9 = (f32[64,128]{1,0:T(8,128)S(1)}, f32[64,128]{1,0:T(8,128)S(1)}, u32[]{:S(2)}, u32[]{:S(2)}) collective-permute-start(f32[64,128]{1,0:T(8,128)S(1)} %project_y.1.refs_0_), channel_id=1, source_target_pairs={{0,12},{4,0},{8,4},{12,8},{1,13},{5,1},{9,5},{13,9},{2,14},{6,2},{... | collective-permute-start | bytes 98312 | tf_op jit(solution)/shard_map/ppermute | solution.py:467
  33.6 1.9 %adjoint.1 = f32[768,128]{1,0:T(8,128)} custom-call(f32[72,128]{1,0:T(8,128)S(1)} %add_add_fusion.refs_0_, f32[72,128]{1,0:T(8,128)S(1)} %collective-permute-done.13.refs_1_, f32[72,128]{1,0:T(8,128)S(1)} %collective-permute-done.14.refs_2_, f32[72,128]{1,0:T(8,128)S(1)} %collective-permute-done.15.refs_3_, f32[1024,256]{1,0:T(8,128)S(1)} %get-tuple-element.34.refs_4_, ...), custom_call_target="tpu_custom_call" | custom-call | tf_op jit(solution)/shard_map/adjoint/pallas_call | solution.py:60
  35.5 1.2 %project_x.1 = f32[2,2,2,64,64]{4,3,2,1,0:T(8,128)} custom-call(f32[64,128]{1,0:T(8,128)S(1)} %project_y.1.refs_0_, f32[64,128]{1,0:T(8,128)S(1)} %collective-permute-done.7.refs_1_, f32[64,128]{1,0:T(8,128)S(1)} %collective-permute-done.8.refs_2_, f32[64,128]{1,0:T(8,128)S(1)} %collective-permute-done.9.refs_3_), custom_call_target="tpu_custom_call" | custom-call | tf_op jit(solution)/shard_map/project_x/pallas_call | solution.py:60
  (17 shorter events, 0.1 us)
Async XLA Ops:
  2.3 6.5 %collective-permute-start = (f32[216,128]{1,0:T(8,128)S(1)}, f32[216,128]{1,0:T(8,128)S(1)}, u32[]{:S(2)}, u32[]{:S(2)}) collective-permute-start(f32[216,128]{1,0:T(8,128)S(1)} %get-tuple-element.21), channel_id=1, source_target_pairs={{0,4},{4,8},{8,12},{12,0},{1,5},{5,9},{9,13},{13,1},{2,6},{6,10},{... | collective-permute-start | bytes 331784 | tf_op jit(solution)/shard_map/ppermute | solution.py:467
  2.8 6.0 %collective-permute-start.1 = (f32[168,128]{1,0:T(8,128)S(1)}, f32[168,128]{1,0:T(8,128)S(1)}, u32[]{:S(2)}, u32[]{:S(2)}) collective-permute-start(f32[168,128]{1,0:T(8,128)S(1)} %get-tuple-element.22), channel_id=1, source_target_pairs={{0,12},{4,0},{8,4},{12,8},{1,13},{5,1},{9,5},{13,9},{2,14},{6,2},{... | collective-permute-start | bytes 258056 | tf_op jit(solution)/shard_map/ppermute | solution.py:467
  6.3 14.2 %collective-permute-start.12 = (f32[72,128]{1,0:T(8,128)S(1)}, f32[72,128]{1,0:T(8,128)S(1)}, u32[]{:S(2)}, u32[]{:S(2)}) collective-permute-start(f32[72,128]{1,0:T(8,128)S(1)} %get-tuple-element.33), channel_id=1, source_target_pairs={{0,12},{4,0},{8,4},{12,8},{1,13},{5,1},{9,5},{13,9},{2,14},{6,2},{... | collective-permute-start | bytes 110600 | tf_op jit(solution)/shard_map/ppermute | solution.py:467
  7.0 13.5 %collective-permute-start.11 = (f32[72,128]{1,0:T(8,128)S(1)}, f32[72,128]{1,0:T(8,128)S(1)}, u32[]{:S(2)}, u32[]{:S(2)}) collective-permute-start(f32[72,128]{1,0:T(8,128)S(1)} %get-tuple-element.32), channel_id=1, source_target_pairs={{0,8},{4,12},{8,0},{12,4},{1,9},{5,13},{9,1},{13,5},{2,10},{6,14},... | collective-permute-start | bytes 110600 | tf_op jit(solution)/shard_map/ppermute | solution.py:467
  8.6 11.9 %collective-permute-start.10 = (f32[72,128]{1,0:T(8,128)S(1)}, f32[72,128]{1,0:T(8,128)S(1)}, u32[]{:S(2)}, u32[]{:S(2)}) collective-permute-start(f32[72,128]{1,0:T(8,128)S(1)} %get-tuple-element.31), channel_id=1, source_target_pairs={{0,4},{4,8},{8,12},{12,0},{1,5},{5,9},{9,13},{13,1},{2,6},{6,10},{... | collective-permute-start | bytes 110600 | tf_op jit(solution)/shard_map/ppermute | solution.py:467
  8.9 5.7 %collective-permute-start.2 = (f32[48,128]{1,0:T(8,128)S(1)}, f32[48,128]{1,0:T(8,128)S(1)}, u32[]{:S(2)}, u32[]{:S(2)}) collective-permute-start(f32[48,128]{1,0:T(8,128)S(1)} %get-tuple-element.25), channel_id=1, source_target_pairs={{0,1},{1,2},{2,3},{3,0},{4,5},{5,6},{6,7},{7,4},{8,9},{9,10},{10,1... | collective-permute-start | bytes 73736 | tf_op jit(solution)/shard_map/ppermute | solution.py:467
  10.5 4.2 %collective-permute-start.3 = (f32[48,128]{1,0:T(8,128)S(1)}, f32[48,128]{1,0:T(8,128)S(1)}, u32[]{:S(2)}, u32[]{:S(2)}) collective-permute-start(f32[48,128]{1,0:T(8,128)S(1)} %get-tuple-element.26), channel_id=1, source_target_pairs={{0,3},{1,0},{2,1},{3,2},{4,7},{5,4},{6,5},{7,6},{8,11},{9,8},{10,9... | collective-permute-start | bytes 73736 | tf_op jit(solution)/shard_map/ppermute | solution.py:467
  19.3 7.2 %collective-permute-start.4 = (f32[64,128]{1,0:T(8,128)S(1)}, f32[64,128]{1,0:T(8,128)S(1)}, u32[]{:S(2)}, u32[]{:S(2)}) collective-permute-start(f32[64,128]{1,0:T(8,128)S(1)} %get-tuple-element.28.refs_0_), channel_id=1, source_target_pairs={{0,1},{1,2},{2,3},{3,0},{4,5},{5,6},{6,7},{7,4},{8,9},{9,10},{10,1... | collective-permute-start | bytes 98312 | tf_op jit(solution)/shard_map/ppermute | solution.py:467
  20.5 11.6 %collective-permute-start.13 = (f32[72,128]{1,0:T(8,128)S(1)}, f32[72,128]{1,0:T(8,128)S(1)}, u32[]{:S(2)}, u32[]{:S(2)}) collective-permute-start(f32[72,128]{1,0:T(8,128)S(1)} %add_add_fusion.refs_0_), channel_id=1, source_target_pairs={{0,1},{1,2},{2,3},{3,0},{4,5},{5,6},{6,7},{7,4},{8,9},{9,10},{10,1... | collective-permute-start | bytes 110600 | tf_op jit(solution)/shard_map/ppermute | solution.py:467
  22.2 7.8 %collective-permute-start.5 = (f32[64,128]{1,0:T(8,128)S(1)}, f32[64,128]{1,0:T(8,128)S(1)}, u32[]{:S(2)}, u32[]{:S(2)}) collective-permute-start(f32[64,128]{1,0:T(8,128)S(1)} %get-tuple-element.28.refs_0_), channel_id=1, source_target_pairs={{0,2},{1,3},{2,0},{3,1},{4,6},{5,7},{6,4},{7,5},{8,10},{9,11},{10,... | collective-permute-start | bytes 98312 | tf_op jit(solution)/shard_map/ppermute | solution.py:467
  23.8 6.2 %collective-permute-start.6 = (f32[64,128]{1,0:T(8,128)S(1)}, f32[64,128]{1,0:T(8,128)S(1)}, u32[]{:S(2)}, u32[]{:S(2)}) collective-permute-start(f32[64,128]{1,0:T(8,128)S(1)} %get-tuple-element.28.refs_0_), channel_id=1, source_target_pairs={{0,3},{1,0},{2,1},{3,2},{4,7},{5,4},{6,5},{7,6},{8,11},{9,8},{10,9... | collective-permute-start | bytes 98312 | tf_op jit(solution)/shard_map/ppermute | solution.py:467
  26.5 7.0 %collective-permute-start.14 = (f32[72,128]{1,0:T(8,128)S(1)}, f32[72,128]{1,0:T(8,128)S(1)}, u32[]{:S(2)}, u32[]{:S(2)}) collective-permute-start(f32[72,128]{1,0:T(8,128)S(1)} %add_add_fusion.refs_0_), channel_id=1, source_target_pairs={{0,2},{1,3},{2,0},{3,1},{4,6},{5,7},{6,4},{7,5},{8,10},{9,11},{10,... | collective-permute-start | bytes 110600 | tf_op jit(solution)/shard_map/ppermute | solution.py:467
  26.5 7.0 %collective-permute-start.15 = (f32[72,128]{1,0:T(8,128)S(1)}, f32[72,128]{1,0:T(8,128)S(1)}, u32[]{:S(2)}, u32[]{:S(2)}) collective-permute-start(f32[72,128]{1,0:T(8,128)S(1)} %add_add_fusion.refs_0_), channel_id=1, source_target_pairs={{0,3},{1,0},{2,1},{3,2},{4,7},{5,4},{6,5},{7,6},{8,11},{9,8},{10,9... | collective-permute-start | bytes 110600 | tf_op jit(solution)/shard_map/ppermute | solution.py:467
  30.5 5.0 %collective-permute-start.7 = (f32[64,128]{1,0:T(8,128)S(1)}, f32[64,128]{1,0:T(8,128)S(1)}, u32[]{:S(2)}, u32[]{:S(2)}) collective-permute-start(f32[64,128]{1,0:T(8,128)S(1)} %project_y.1.refs_0_), channel_id=1, source_target_pairs={{0,4},{4,8},{8,12},{12,0},{1,5},{5,9},{9,13},{13,1},{2,6},{6,10},{... | collective-permute-start | bytes 98312 | tf_op jit(solution)/shard_map/ppermute | solution.py:467
  30.6 5.0 %collective-permute-start.8 = (f32[64,128]{1,0:T(8,128)S(1)}, f32[64,128]{1,0:T(8,128)S(1)}, u32[]{:S(2)}, u32[]{:S(2)}) collective-permute-start(f32[64,128]{1,0:T(8,128)S(1)} %project_y.1.refs_0_), channel_id=1, source_target_pairs={{0,8},{4,12},{8,0},{12,4},{1,9},{5,13},{9,1},{13,5},{2,10},{6,14},... | collective-permute-start | bytes 98312 | tf_op jit(solution)/shard_map/ppermute | solution.py:467
  32.2 3.4 %collective-permute-start.9 = (f32[64,128]{1,0:T(8,128)S(1)}, f32[64,128]{1,0:T(8,128)S(1)}, u32[]{:S(2)}, u32[]{:S(2)}) collective-permute-start(f32[64,128]{1,0:T(8,128)S(1)} %project_y.1.refs_0_), channel_id=1, source_target_pairs={{0,12},{4,0},{8,4},{12,8},{1,13},{5,1},{9,5},{13,9},{2,14},{6,2},{... | collective-permute-start | bytes 98312 | tf_op jit(solution)/shard_map/ppermute | solution.py:467
